TPU v7x, 32 devices: a whole 2x2x4 slice. The times are simulated.
32 devices in a mesh: dp: 4 (over z), ctx: 2 (over y), tp: 4 (over x, core).
Axes of the slice: x: 2, y: 2, z: 4, core: 2. Of those that a mesh axis runs over, the one named last changes fastest.
Arguments:
- inputs: bfloat16 [8, 1024, 768], P('dp', ('ctx', 'tp')), may hold values from -6 to 6
- segments: int32 [8, 1024], P('dp', 'ctx'), may hold values from 0 to 4, never falling along the last dimension, each value on 1 to 512 neighbouring positions
- cotangent: bfloat16 [8, 1024, 768], P('dp', ('ctx', 'tp')), may hold values from -6 to 6
- student_first_gain: bfloat16 [768], P('dp'), may hold values from 0.5 to 1.5
- student_first_shift: bfloat16 [768], P('dp'), may hold values from -3 to 3
- student_merged_weight: bfloat16 [768, 3, 768], P('dp', None, 'tp'), may hold values from -0.21875 to 0.21875
- student_merged_bias: bfloat16 [2, 12, 64], P(None, 'tp', 'dp'), may hold values from -3 to 3
- student_output_weight: bfloat16 [768, 768], P('tp', 'dp'), may hold values from -1.25 to 1.25
- student_output_bias: bfloat16 [768], P('dp'), may hold values from -3 to 3
- student_second_gain: bfloat16 [768], P('dp'), may hold values from 0.5 to 1.5
- student_second_shift: bfloat16 [768], P('dp'), may hold values from -3 to 3
- student_expand_weight: bfloat16 [768, 3072], P('dp', 'tp'), may hold values from -0.21875 to 0.21875
- student_expand_bias: bfloat16 [48, 64], P('tp', 'dp'), may hold values from -3 to 3
- student_reduce_weight: bfloat16 [3072, 768], P('tp', 'dp'), may hold values from -0.109375 to 0.109375
- student_reduce_bias: bfloat16 [768], P('dp'), may hold values from -3 to 3
- teacher_first_gain: bfloat16 [768], P('dp'), may hold values from 0.5 to 1.5
- teacher_first_shift: bfloat16 [768], P('dp'), may hold values from -3 to 3
- teacher_merged_weight: bfloat16 [768, 3, 768], P('dp', None, 'tp'), may hold values from -0.21875 to 0.21875
- teacher_merged_bias: bfloat16 [2, 12, 64], P(None, 'tp', 'dp'), may hold values from -3 to 3
- teacher_output_weight: bfloat16 [768, 768], P('tp', 'dp'), may hold values from -1.25 to 1.25
- teacher_output_bias: bfloat16 [768], P('dp'), may hold values from -3 to 3
- teacher_second_gain: bfloat16 [768], P('dp'), may hold values from 0.5 to 1.5
- teacher_second_shift: bfloat16 [768], P('dp'), may hold values from -3 to 3
- teacher_expand_weight: bfloat16 [768, 3072], P('dp', 'tp'), may hold values from -0.21875 to 0.21875
- teacher_expand_bias: bfloat16 [48, 64], P('tp', 'dp'), may hold values from -3 to 3
- teacher_reduce_weight: bfloat16 [3072, 768], P('tp', 'dp'), may hold values from -0.109375 to 0.109375
- teacher_reduce_bias: bfloat16 [768], P('dp'), may hold values from -3 to 3
Outputs:
- output: bfloat16 [8, 1024, 768], P('dp', ('ctx', 'tp'))
- input_grad: float32 [8, 1024, 768], P('dp', ('ctx', 'tp'))
- grad_student_first_gain: float32 [768], P('dp')
- grad_student_first_shift: float32 [768], P('dp')
- grad_student_merged_weight: float32 [768, 3, 768], P('dp', None, 'tp')
- grad_student_merged_bias: float32 [2, 12, 64], P(None, 'tp', 'dp')
- grad_student_output_weight: float32 [768, 768], P('tp', 'dp')
- grad_student_output_bias: float32 [768], P('dp')
- grad_student_second_gain: float32 [768], P('dp')
- grad_student_second_shift: float32 [768], P('dp')
- grad_student_expand_weight: float32 [768, 3072], P('dp', 'tp')
- grad_student_expand_bias: float32 [48, 64], P('tp', 'dp')
- grad_student_reduce_weight: float32 [3072, 768], P('tp', 'dp')
- grad_student_reduce_bias: float32 [768], P('dp')
- grad_teacher_first_gain: float32 [768], P('dp')
- grad_teacher_first_shift: float32 [768], P('dp')
- grad_teacher_merged_weight: float32 [768, 3, 768], P('dp', None, 'tp')
- grad_teacher_merged_bias: float32 [2, 12, 64], P(None, 'tp', 'dp')
- grad_teacher_output_weight: float32 [768, 768], P('tp', 'dp')
- grad_teacher_output_bias: float32 [768], P('dp')
- grad_teacher_second_gain: float32 [768], P('dp')
- grad_teacher_second_shift: float32 [768], P('dp')
- grad_teacher_expand_weight: float32 [768, 3072], P('dp', 'tp')
- grad_teacher_expand_bias: float32 [48, 64], P('tp', 'dp')
- grad_teacher_reduce_weight: float32 [3072, 768], P('tp', 'dp')
- grad_teacher_reduce_bias: float32 [768], P('dp')
Inputs may be any that keep to these rules, and one draw needn't show every extreme that they name: `segments`: within a sequence the document numbers never fall from one token to the next; a document holds 1 to 512 consecutive tokens, and each sequence has one of exactly 512.
All inputs are finite; a program needn't handle non-finite values.
Results may differ from a plain program's by a relative error of at most 0.025.
Values may be sent and summed in bfloat16 or wider, within the bound.
No kernel may reach another device: no remote copies, remote signals or barrier semaphores. Data moves between devices by JAX's collectives and lax.ppermute only.
A program may use at most 192 MiB of HBM per device.

v0:
```python
import jax
import jax.numpy as jnp
from jax import lax
from jax.sharding import PartitionSpec as P

HD = 64
DOC_MAX = 2000


EPSILON = 1e-05
GELU_SCALE = 0.7978845608028654


def from_behind(block, axis, distance):
    devices = range(lax.axis_size(axis))
    route = [(i - distance, i) for i in devices if i - distance in devices]
    return lax.ppermute(block, axis, route)


def layer_norm(values, norm_gain, norm_shift):
    center = values - jnp.mean(values, axis=-1, keepdims=True)
    spread = jnp.mean(center * center, axis=-1, keepdims=True)
    return center * lax.rsqrt(spread + EPSILON) * norm_gain + norm_shift


def gelu_tanh(values):
    return (
        0.5 * values * (1.0 + jnp.tanh(GELU_SCALE * (values + 0.044715 * values * values * values)))
    )


def spread_rows(row_block):
    return lax.all_gather(row_block, "tp", axis=1, tiled=True)


def gather_sums(partial_value):
    return lax.psum_scatter(
        partial_value.astype(jnp.bfloat16), "tp", scatter_dimension=1, tiled=True
    ).astype(jnp.float32)


def to_items(tensor, head_count):
    batches, length, features = tensor.shape
    head_size = features // head_count
    return (
        tensor.reshape(batches, length, head_count, head_size)
        .transpose(0, 2, 1, 3)
        .reshape(batches * head_count, length, head_size)
    )


def from_items(tensor, head_count):
    item_count, length, head_size = tensor.shape
    batches = item_count // head_count
    return (
        tensor.reshape(batches, head_count, length, head_size)
        .transpose(0, 2, 1, 3)
        .reshape(batches, length, head_count * head_size)
    )


def masked_scores(query_rows, key_rows, query_docs, key_docs, allowed):
    raw_scores = (
        jnp.einsum("qd,kd->qk", query_rows, key_rows, preferred_element_type=jnp.float32) * 0.125
    )
    keep_mask = allowed & (key_docs[None, :] == query_docs[:, None])
    return (jnp.where(keep_mask, raw_scores, -1e30), keep_mask)


def attend_forward(allowed):

    def attend_item(packed):
        query_rows, key_rows, value_rows, query_docs, key_docs = packed
        scores, keep_mask = masked_scores(query_rows, key_rows, query_docs, key_docs, allowed)
        row_top = jnp.max(scores, axis=-1, keepdims=True)
        raised = jnp.exp(scores - row_top)
        row_total = jnp.sum(raised, axis=-1, keepdims=True)
        weights = (raised / row_total).astype(jnp.bfloat16)
        mixed_rows = jnp.dot(weights, value_rows, preferred_element_type=jnp.float32).astype(
            jnp.bfloat16
        )
        return (mixed_rows, row_top[:, 0] + jnp.log(row_total[:, 0]))

    return attend_item


def attend_backward(allowed):

    def attend_item(packed):
        query_rows, key_rows, value_rows, query_docs, key_docs, log_total, grad_rows = packed
        scores, keep_mask = masked_scores(query_rows, key_rows, query_docs, key_docs, allowed)
        weights = jnp.where(keep_mask, jnp.exp(scores - log_total[:, None]), 0.0)
        grad_values = jnp.einsum(
            "qk,qd->kd", weights.astype(jnp.bfloat16), grad_rows, preferred_element_type=jnp.float32
        )
        grad_weights = jnp.einsum(
            "qd,kd->qk", grad_rows, value_rows, preferred_element_type=jnp.float32
        )
        centered = jnp.sum(weights * grad_weights, axis=-1, keepdims=True)
        grad_scores = (weights * (grad_weights - centered)).astype(jnp.bfloat16)
        grad_query = jnp.dot(grad_scores, key_rows, preferred_element_type=jnp.float32) * 0.125
        grad_keys = (
            jnp.einsum("qk,qd->kd", grad_scores, query_rows, preferred_element_type=jnp.float32)
            * 0.125
        )
        return (grad_query, grad_keys, grad_values)

    return attend_item


def layer_forward(stream, params, segments, key_docs, allowed, cycle_steps):
    (
        first_gain,
        first_shift,
        merged_weight,
        merged_bias,
        output_weight,
        output_bias,
        second_gain,
        second_shift,
        expand_weight,
        expand_bias,
        reduce_weight,
        reduce_bias,
    ) = params
    fetched = (
        lax.all_gather(first_gain, "dp", axis=0, tiled=True),
        lax.all_gather(first_shift, "dp", axis=0, tiled=True),
        lax.all_gather(merged_weight, "dp", axis=0, tiled=True),
        lax.all_gather(merged_bias, "dp", axis=2, tiled=True),
        lax.all_gather(output_weight, "dp", axis=1, tiled=True),
        lax.all_gather(output_bias, "dp", axis=0, tiled=True),
        lax.all_gather(second_gain, "dp", axis=0, tiled=True),
        lax.all_gather(second_shift, "dp", axis=0, tiled=True),
        lax.all_gather(expand_weight, "dp", axis=0, tiled=True),
        lax.all_gather(expand_bias, "dp", axis=1, tiled=True),
        lax.all_gather(reduce_weight, "dp", axis=1, tiled=True),
        lax.all_gather(reduce_bias, "dp", axis=0, tiled=True),
    )
    (
        first_gain,
        first_shift,
        merged_weight,
        merged_bias,
        output_weight,
        output_bias,
        second_gain,
        second_shift,
        expand_weight,
        expand_bias,
        reduce_weight,
        reduce_bias,
    ) = fetched
    head_count = merged_weight.shape[2] // HD
    normed = layer_norm(
        stream, first_gain.astype(jnp.float32), first_shift.astype(jnp.float32)
    ).astype(jnp.bfloat16)
    first_rows = spread_rows(normed)
    merged_out = jnp.einsum(
        "std,dkf->stkf", first_rows, merged_weight, preferred_element_type=jnp.float32
    )
    bias_pair = merged_bias.astype(jnp.float32).reshape(2, -1)
    query_rows = (merged_out[:, :, 0] + bias_pair[0]).astype(jnp.bfloat16)
    key_rows = merged_out[:, :, 1].astype(jnp.bfloat16)
    value_rows = (merged_out[:, :, 2] + bias_pair[1]).astype(jnp.bfloat16)
    key_list = [key_rows]
    value_list = [value_rows]
    moving = (key_rows, value_rows)
    for offset in range(cycle_steps):
        moving = from_behind((moving[0], moving[1]), "ctx", 1)
        key_list.insert(0, moving[0])
        value_list.insert(0, moving[1])
    query_items = to_items(query_rows, head_count)
    key_items = to_items(jnp.concatenate(key_list, axis=1), head_count)
    value_items = to_items(jnp.concatenate(value_list, axis=1), head_count)
    query_docs = jnp.repeat(segments, head_count, axis=0)
    window_docs = jnp.repeat(key_docs, head_count, axis=0)
    mixed_items, log_total = lax.map(
        attend_forward(allowed), (query_items, key_items, value_items, query_docs, window_docs)
    )
    mixed = from_items(mixed_items, head_count)
    attn_part = jnp.einsum("stf,fd->std", mixed, output_weight, preferred_element_type=jnp.float32)
    middle = stream + gather_sums(attn_part) + output_bias.astype(jnp.float32)
    normed_two = layer_norm(
        middle, second_gain.astype(jnp.float32), second_shift.astype(jnp.float32)
    ).astype(jnp.bfloat16)
    second_rows = spread_rows(normed_two)
    hidden = jnp.einsum(
        "std,df->stf", second_rows, expand_weight, preferred_element_type=jnp.float32
    ) + expand_bias.astype(jnp.float32).reshape(-1)
    activated = gelu_tanh(hidden).astype(jnp.bfloat16)
    mlp_part = jnp.einsum(
        "stf,fd->std", activated, reduce_weight, preferred_element_type=jnp.float32
    )
    result = middle + gather_sums(mlp_part) + reduce_bias.astype(jnp.float32)
    saved_state = (
        fetched,
        stream,
        first_rows,
        query_items,
        key_items,
        value_items,
        query_docs,
        window_docs,
        log_total,
        mixed,
        middle,
        second_rows,
        hidden,
        activated,
    )
    return (result, saved_state)


def reduce_grads(fresh):
    (
        gain_one,
        shift_one,
        merged_weights,
        merged_biases,
        output_weights,
        output_biases,
        gain_two,
        shift_two,
        expand_weights,
        expand_biases,
        reduce_weights,
        reduce_biases,
    ) = fresh
    summed = (
        lax.psum(gain_one.astype(jnp.bfloat16), "ctx").astype(jnp.float32),
        lax.psum(shift_one.astype(jnp.bfloat16), "ctx").astype(jnp.float32),
        lax.psum(merged_weights.astype(jnp.bfloat16), "ctx").astype(jnp.float32),
        lax.psum(merged_biases.astype(jnp.bfloat16), "ctx").astype(jnp.float32),
        lax.psum(output_weights.astype(jnp.bfloat16), "ctx").astype(jnp.float32),
        lax.psum(output_biases.astype(jnp.bfloat16), "ctx").astype(jnp.float32),
        lax.psum(gain_two.astype(jnp.bfloat16), "ctx").astype(jnp.float32),
        lax.psum(shift_two.astype(jnp.bfloat16), "ctx").astype(jnp.float32),
        lax.psum(expand_weights.astype(jnp.bfloat16), "ctx").astype(jnp.float32),
        lax.psum(expand_biases.astype(jnp.bfloat16), "ctx").astype(jnp.float32),
        lax.psum(reduce_weights.astype(jnp.bfloat16), "ctx").astype(jnp.float32),
        lax.psum(reduce_biases.astype(jnp.bfloat16), "ctx").astype(jnp.float32),
    )
    (
        gain_one,
        shift_one,
        merged_weights,
        merged_biases,
        output_weights,
        output_biases,
        gain_two,
        shift_two,
        expand_weights,
        expand_biases,
        reduce_weights,
        reduce_biases,
    ) = summed
    return (
        lax.psum_scatter(
            gain_one.astype(jnp.bfloat16), "dp", scatter_dimension=0, tiled=True
        ).astype(jnp.float32),
        lax.psum_scatter(
            shift_one.astype(jnp.bfloat16), "dp", scatter_dimension=0, tiled=True
        ).astype(jnp.float32),
        lax.psum_scatter(
            merged_weights.astype(jnp.bfloat16), "dp", scatter_dimension=0, tiled=True
        ).astype(jnp.float32),
        lax.psum_scatter(
            merged_biases.astype(jnp.bfloat16), "dp", scatter_dimension=2, tiled=True
        ).astype(jnp.float32),
        lax.psum_scatter(
            output_weights.astype(jnp.bfloat16), "dp", scatter_dimension=1, tiled=True
        ).astype(jnp.float32),
        lax.psum_scatter(
            output_biases.astype(jnp.bfloat16), "dp", scatter_dimension=0, tiled=True
        ).astype(jnp.float32),
        lax.psum_scatter(
            gain_two.astype(jnp.bfloat16), "dp", scatter_dimension=0, tiled=True
        ).astype(jnp.float32),
        lax.psum_scatter(
            shift_two.astype(jnp.bfloat16), "dp", scatter_dimension=0, tiled=True
        ).astype(jnp.float32),
        lax.psum_scatter(
            expand_weights.astype(jnp.bfloat16), "dp", scatter_dimension=0, tiled=True
        ).astype(jnp.float32),
        lax.psum_scatter(
            expand_biases.astype(jnp.bfloat16), "dp", scatter_dimension=1, tiled=True
        ).astype(jnp.float32),
        lax.psum_scatter(
            reduce_weights.astype(jnp.bfloat16), "dp", scatter_dimension=1, tiled=True
        ).astype(jnp.float32),
        lax.psum_scatter(
            reduce_biases.astype(jnp.bfloat16), "dp", scatter_dimension=0, tiled=True
        ).astype(jnp.float32),
    )


def layer_backward(grad_out, saved_state, allowed, cycle_steps, token_count):
    (
        fetched,
        stream,
        first_rows,
        query_items,
        key_items,
        value_items,
        query_docs,
        window_docs,
        log_total,
        mixed,
        middle,
        second_rows,
        hidden,
        activated,
    ) = saved_state
    (
        first_gain,
        first_shift,
        merged_weight,
        merged_bias,
        output_weight,
        output_bias,
        second_gain,
        second_shift,
        expand_weight,
        expand_bias,
        reduce_weight,
        reduce_bias,
    ) = fetched
    head_count = merged_weight.shape[2] // HD
    grad_branch = spread_rows(grad_out.astype(jnp.bfloat16))
    grad_reduce = jnp.einsum(
        "stf,std->fd", activated, grad_branch, preferred_element_type=jnp.float32
    )
    grad_active = jnp.einsum(
        "std,fd->stf", grad_branch, reduce_weight, preferred_element_type=jnp.float32
    )
    _, gelu_pull = jax.vjp(gelu_tanh, hidden)
    grad_hidden = gelu_pull(grad_active)[0].astype(jnp.bfloat16)
    grad_expand_bias = jnp.sum(grad_hidden, axis=(0, 1), dtype=jnp.float32).reshape(
        expand_bias.shape
    )
    grad_expand = jnp.einsum(
        "std,stf->df", second_rows, grad_hidden, preferred_element_type=jnp.float32
    )
    grad_second = gather_sums(
        jnp.einsum("stf,df->std", grad_hidden, expand_weight, preferred_element_type=jnp.float32)
    )
    _, second_pull = jax.vjp(
        layer_norm, middle, second_gain.astype(jnp.float32), second_shift.astype(jnp.float32)
    )
    grad_norm_mid, grad_second_gain, grad_second_shift = second_pull(grad_second)
    grad_middle = grad_out + grad_norm_mid
    grad_reduce_bias = jnp.sum(grad_out, axis=(0, 1))
    grad_attend = spread_rows(grad_middle.astype(jnp.bfloat16))
    grad_output = jnp.einsum("stf,std->fd", mixed, grad_attend, preferred_element_type=jnp.float32)
    grad_mixed = jnp.einsum(
        "std,fd->stf", grad_attend, output_weight, preferred_element_type=jnp.float32
    ).astype(jnp.bfloat16)
    grad_query_items, grad_key_items, grad_value_items = lax.map(
        attend_backward(allowed),
        (
            query_items,
            key_items,
            value_items,
            query_docs,
            window_docs,
            log_total,
            to_items(grad_mixed, head_count),
        ),
    )
    grad_query = from_items(grad_query_items, head_count)
    window_keys = from_items(grad_key_items, head_count)
    window_values = from_items(grad_value_items, head_count)
    local_keys = window_keys[:, cycle_steps * token_count :]
    local_values = window_values[:, cycle_steps * token_count :]
    carried = None
    for offset in range(cycle_steps, 0, -1):
        start_row = (cycle_steps - offset) * token_count
        block_keys = window_keys[:, start_row : start_row + token_count]
        block_values = window_values[:, start_row : start_row + token_count]
        if carried is not None:
            block_keys = block_keys + carried[0]
            block_values = block_values + carried[1]
        carried = (
            from_behind(block_keys.astype(jnp.bfloat16), "ctx", -1).astype(block_keys.dtype),
            from_behind(block_values.astype(jnp.bfloat16), "ctx", -1).astype(block_values.dtype),
        )
    local_keys = local_keys + carried[0]
    local_values = local_values + carried[1]
    grad_merged = jnp.stack([grad_query, local_keys, local_values], axis=2).astype(jnp.bfloat16)
    grad_merged_bias = jnp.stack(
        [
            jnp.sum(grad_merged[:, :, 0], axis=(0, 1), dtype=jnp.float32),
            jnp.sum(grad_merged[:, :, 2], axis=(0, 1), dtype=jnp.float32),
        ]
    ).reshape(merged_bias.shape)
    grad_merged_weight = jnp.einsum(
        "std,stkf->dkf", first_rows, grad_merged, preferred_element_type=jnp.float32
    )
    grad_first = gather_sums(
        jnp.einsum("stkf,dkf->std", grad_merged, merged_weight, preferred_element_type=jnp.float32)
    )
    _, first_pull = jax.vjp(
        layer_norm, stream, first_gain.astype(jnp.float32), first_shift.astype(jnp.float32)
    )
    grad_norm_in, grad_first_gain, grad_first_shift = first_pull(grad_first)
    grad_input = grad_middle + grad_norm_in
    grad_output_bias = jnp.sum(grad_middle, axis=(0, 1))
    vector_grads = lax.psum(
        (
            grad_first_gain,
            grad_first_shift,
            grad_second_gain,
            grad_second_shift,
            grad_output_bias,
            grad_reduce_bias,
        ),
        "tp",
    )
    fresh = (
        vector_grads[0],
        vector_grads[1],
        grad_merged_weight,
        grad_merged_bias,
        grad_output,
        vector_grads[4],
        vector_grads[2],
        vector_grads[3],
        grad_expand,
        grad_expand_bias,
        grad_reduce,
        vector_grads[5],
    )
    return (grad_input, reduce_grads(fresh))


def shards(
    inputs,
    segments,
    cotangent,
    student_first_gain,
    student_first_shift,
    student_merged_weight,
    student_merged_bias,
    student_output_weight,
    student_output_bias,
    student_second_gain,
    student_second_shift,
    student_expand_weight,
    student_expand_bias,
    student_reduce_weight,
    student_reduce_bias,
    teacher_first_gain,
    teacher_first_shift,
    teacher_merged_weight,
    teacher_merged_bias,
    teacher_output_weight,
    teacher_output_bias,
    teacher_second_gain,
    teacher_second_shift,
    teacher_expand_weight,
    teacher_expand_bias,
    teacher_reduce_weight,
    teacher_reduce_bias,
):
    student = (
        student_first_gain,
        student_first_shift,
        student_merged_weight,
        student_merged_bias,
        student_output_weight,
        student_output_bias,
        student_second_gain,
        student_second_shift,
        student_expand_weight,
        student_expand_bias,
        student_reduce_weight,
        student_reduce_bias,
    )
    teacher = (
        teacher_first_gain,
        teacher_first_shift,
        teacher_merged_weight,
        teacher_merged_bias,
        teacher_output_weight,
        teacher_output_bias,
        teacher_second_gain,
        teacher_second_shift,
        teacher_expand_weight,
        teacher_expand_bias,
        teacher_reduce_weight,
        teacher_reduce_bias,
    )
    token_count = segments.shape[1]
    context_size = lax.axis_size("ctx")
    context_index = lax.axis_index("ctx")
    doc_long = min(DOC_MAX, token_count * context_size // 2)
    cycle_steps = min((doc_long - 2) // token_count + 1, context_size - 1)
    doc_list = [segments]
    moving = segments
    for offset in range(cycle_steps):
        moving = from_behind(moving, "ctx", 1)
        doc_list.insert(0, moving)
    key_docs = jnp.concatenate(doc_list, axis=1)
    places = jnp.arange((cycle_steps + 1) * token_count, dtype=jnp.int32)
    relative = places - cycle_steps * token_count
    source = cycle_steps - places // token_count
    query_place = jnp.arange(token_count, dtype=jnp.int32)
    allowed = (relative[None, :] <= query_place[:, None]) & (source <= context_index)[None, :]
    stream = inputs.astype(jnp.float32)
    middle_stream, student_saved = layer_forward(
        stream, student, segments, key_docs, allowed, cycle_steps
    )
    final_stream, teacher_saved = layer_forward(
        middle_stream, teacher, segments, key_docs, allowed, cycle_steps
    )
    teacher_in_grad, teacher_grads = layer_backward(
        cotangent.astype(jnp.float32), teacher_saved, allowed, cycle_steps, token_count
    )
    input_grad, student_grads = layer_backward(
        teacher_in_grad, student_saved, allowed, cycle_steps, token_count
    )
    return (
        (final_stream.astype(jnp.bfloat16), input_grad)
        + tuple(student_grads)
        + tuple(teacher_grads)
    )


def solution(mesh):
    placed = (
        P("dp", ("ctx", "tp"), None),
        P("dp", "ctx"),
        P("dp", ("ctx", "tp"), None),
        P("dp"),
        P("dp"),
        P("dp", None, "tp"),
        P(None, "tp", "dp"),
        P("tp", "dp"),
        P("dp"),
        P("dp"),
        P("dp"),
        P("dp", "tp"),
        P("tp", "dp"),
        P("tp", "dp"),
        P("dp"),
        P("dp"),
        P("dp"),
        P("dp", None, "tp"),
        P(None, "tp", "dp"),
        P("tp", "dp"),
        P("dp"),
        P("dp"),
        P("dp"),
        P("dp", "tp"),
        P("tp", "dp"),
        P("tp", "dp"),
        P("dp"),
    )
    return jax.shard_map(
        shards,
        mesh=mesh,
        in_specs=placed,
        out_specs=(
            P("dp", ("ctx", "tp"), None),
            P("dp", ("ctx", "tp"), None),
            P("dp"),
            P("dp"),
            P("dp", None, "tp"),
            P(None, "tp", "dp"),
            P("tp", "dp"),
            P("dp"),
            P("dp"),
            P("dp"),
            P("dp", "tp"),
            P("tp", "dp"),
            P("tp", "dp"),
            P("dp"),
            P("dp"),
            P("dp"),
            P("dp", None, "tp"),
            P(None, "tp", "dp"),
            P("tp", "dp"),
            P("dp"),
            P("dp"),
            P("dp"),
            P("dp", "tp"),
            P("tp", "dp"),
            P("tp", "dp"),
            P("dp"),
        ),
        check_vma=False,
    )
```

profile of v0, /device:TPU:0, one launch (start us, length us, event | category | flops | bytes accessed | tf_op | source)
XLA Modules:
  0.0 1194.9 jit_solution(14446302358967537211)
XLA Ops:
  19.3 21.3 %all-reduce.26 = (bf16[768]{0:T(1024)(128)(2,1)S(1)}, bf16[768]{0:T(1024)(128)(2,1)S(1)}, bf16[768]{0:T(1024)(128)(2,1)S(1)}, bf16[768]{0:T(1024)(128)(2,1)S(1)}...) all-reduce(bf16[768]{0:T(1024)(128)(2,1)S(1)} %dynamic-update-slice, ...), channel_id=1, replica_groups=mesh['dp'=4,'ctx'=2,'tp'=4] {'dp'}, use_global_device_ids=true, to_apply=%add.1 | all-reduce | flops 8448 | bytes 33792
  45.7 3.4 collective-permute-start
  49.7 13.2 %all_gather.100 = bf16[2,3,64]{1,0,2:T(2,128)(2,1)S(1)} all-gather(bf16[2,3,16]{1,0,2:T(2,128)(2,1)S(1)} %copy.209), channel_id=1, replica_groups=mesh['dp'=4,'ctx'=2,'tp'=4] {'dp'}, dimensions={2}, use_global_device_ids=true | all-gather | bytes 960 | tf_op jit(solution)/shard_map/all_gather | solution.py:130
  63.0 24.3 %all_gather.99 = bf16[768,3,192]{2,1,0:T(4,128)(2,1)S(1)} all-gather(bf16[192,3,192]{2,1,0:T(4,128)(2,1)S(1)} %copy.207), channel_id=1, replica_groups=mesh['dp'=4,'ctx'=2,'tp'=4] {'dp'}, dimensions={0}, use_global_device_ids=true | all-gather | bytes 1105920 | tf_op jit(solution)/shard_map/all_gather | solution.py:129
  87.2 14.3 %all_gather.101 = bf16[192,768]{0,1:T(8,128)(2,1)S(1)} all-gather(bf16[192,192]{0,1:T(8,128)(2,1)S(1)} %copy.218), channel_id=1, replica_groups=mesh['dp'=4,'ctx'=2,'tp'=4] {'dp'}, dimensions={1}, use_global_device_ids=true | all-gather | bytes 368640 | tf_op jit(solution)/shard_map/all_gather | solution.py:131
  109.5 2.7 collective-permute-done.2
  118.1 24.9 %while.56 = (s32[]{:T(128)}, bf16[6,512,64]{1,2,0:T(8,128)(2,1)S(1)}, f32[6,512]{1,0:T(8,128)S(1)}, s32[6,1024]{1,0:T(8,128)S(1)}, s32[6,512]{1,0:T(8,128)S(1)},...) while((s32[]{:T(128)}, ...), condition=%wide.region_5.6_spmd.clone, body=%wide.region_2.5_spmd.clone.sunk | while | flops 140541440 | bytes 7058561 | solution.py:178
  145.6 29.4 %reduce-scatter.33.cloned.1.call-done = bf16[2,128,768]{2,1,0:T(8,128)(2,1)} async-done(((bf16[2,512,768]{2,1,0:T(8,128)(2,1)}), bf16[2,128,768]{2,1,0:T(8,128)(2,1)}) %reduce-scatter.33.cloned.1.call-update) | async-done | bytes 393232 | tf_op jit(solution)/shard_map/reduce_scatter | solution.py:37
  180.2 13.4 %all_gather.107 = bf16[12,64]{0,1:T(8,128)(2,1)S(1)} all-gather(bf16[12,16]{0,1:T(8,128)(2,1)S(1)} %copy.220), channel_id=1, replica_groups=mesh['dp'=4,'ctx'=2,'tp'=4] {'dp'}, dimensions={1}, use_global_device_ids=true | all-gather | bytes 1920 | tf_op jit(solution)/shard_map/all_gather | solution.py:136
  193.7 6.0 all-gather.15.cloned.1.call-done
  199.8 4.8 fusion.124
  204.6 26.9 %all-gather.19.cloned.1.call-done = bf16[768,768]{0,1:T(8,128)(2,1)} async-done(((bf16[768,192]{0,1:T(8,128)(2,1)}), bf16[768,768]{0,1:T(8,128)(2,1)}) %all-gather.19.cloned.1.call-update) | async-done | bytes 1179664 | tf_op jit(solution)/shard_map/all_gather | solution.py:137
  231.5 5.5 convolution_convert_fusion.6
  237.2 27.4 %reduce-scatter.35.cloned.1.call-done = bf16[2,128,768]{2,1,0:T(8,128)(2,1)} async-done(((bf16[2,512,768]{2,1,0:T(8,128)(2,1)}), bf16[2,128,768]{2,1,0:T(8,128)(2,1)}) %reduce-scatter.35.cloned.1.call-update) | async-done | bytes 393232 | tf_op jit(solution)/shard_map/reduce_scatter | solution.py:37
  267.5 29.9 %all_gather.113 = bf16[768,3,192]{2,1,0:T(4,128)(2,1)S(1)} all-gather(bf16[192,3,192]{2,1,0:T(4,128)(2,1)S(1)} %copy.222), channel_id=1, replica_groups=mesh['dp'=4,'ctx'=2,'tp'=4] {'dp'}, dimensions={0}, use_global_device_ids=true | all-gather | bytes 1105920 | tf_op jit(solution)/shard_map/all_gather | solution.py:129
  299.8 13.1 %all_gather.114 = bf16[2,3,64]{1,0,2:T(2,128)(2,1)S(1)} all-gather(bf16[2,3,16]{1,0,2:T(2,128)(2,1)S(1)} %copy.224), channel_id=1, replica_groups=mesh['dp'=4,'ctx'=2,'tp'=4] {'dp'}, dimensions={2}, use_global_device_ids=true | all-gather | bytes 960 | tf_op jit(solution)/shard_map/all_gather | solution.py:130
  313.4 15.8 %all_gather.115 = bf16[192,768]{0,1:T(8,128)(2,1)} all-gather(bf16[192,192]{0,1:T(8,128)(2,1)S(1)} %copy.233), channel_id=1, replica_groups=mesh['dp'=4,'ctx'=2,'tp'=4] {'dp'}, dimensions={1}, use_global_device_ids=true | all-gather | bytes 368640 | tf_op jit(solution)/shard_map/all_gather | solution.py:131
  329.2 2.7 fusion.103
  332.2 3.4 collective-permute-start.4
  338.2 3.5 collective-permute-done.4
  348.4 28.5 %while.57 = (s32[]{:T(128)}, bf16[6,512,64]{1,2,0:T(8,128)(2,1)}, f32[6,512]{1,0:T(8,128)S(1)}, s32[6,1024]{1,0:T(8,128)S(1)}, s32[6,512]{1,0:T(8,128)S(1)}, /*i...) while((s32[]{:T(128)}, bf16[6,512,64]{1,2,0:T(8,128)(2,1)}, ...), condition=%wide.region_15.16_spmd.clone, body=%wide.region_12.15_spmd.clone.sunk | while | flops 140541440 | bytes 7058561 | solution.py:178
  376.9 3.0 convolution_convert_fusion.5
  380.8 29.4 %reduce-scatter.37.cloned.1.call-done = bf16[2,128,768]{2,1,0:T(8,128)(2,1)} async-done(((bf16[2,512,768]{2,1,0:T(8,128)(2,1)}), bf16[2,128,768]{2,1,0:T(8,128)(2,1)}) %reduce-scatter.37.cloned.1.call-update) | async-done | bytes 393232 | tf_op jit(solution)/shard_map/reduce_scatter | solution.py:37
  413.9 13.6 %all_gather.121 = bf16[12,64]{0,1:T(8,128)(2,1)S(1)} all-gather(bf16[12,16]{0,1:T(8,128)(2,1)S(1)} %copy.235), channel_id=1, replica_groups=mesh['dp'=4,'ctx'=2,'tp'=4] {'dp'}, dimensions={1}, use_global_device_ids=true | all-gather | bytes 1920 | tf_op jit(solution)/shard_map/all_gather | solution.py:136
  427.7 14.5 %all-gather.25.cloned.1.call-done = bf16[768,768]{1,0:T(8,128)(2,1)} async-done(((bf16[192,768]{1,0:T(8,128)(2,1)}), bf16[768,768]{1,0:T(8,128)(2,1)}) %all-gather.25.cloned.1.call-update) | async-done | bytes 1179664 | tf_op jit(solution)/shard_map/all_gather | solution.py:135
  442.3 20.8 %all-gather.23.cloned.1.call-done = bf16[2,512,768]{2,1,0:T(8,128)(2,1)} async-done(((bf16[2,128,768]{2,1,0:T(8,128)(2,1)}), bf16[2,512,768]{2,1,0:T(8,128)(2,1)}) %all-gather.23.cloned.1.call-update) | async-done | bytes 1572880 | tf_op jit(solution)/shard_map/all_gather | solution.py:33
  463.0 4.8 fusion.119
  467.8 27.0 %all-gather.27.cloned.1.call-done = bf16[768,768]{0,1:T(8,128)(2,1)} async-done(((bf16[768,192]{0,1:T(8,128)(2,1)}), bf16[768,768]{0,1:T(8,128)(2,1)}) %all-gather.27.cloned.1.call-update) | async-done | bytes 1179664 | tf_op jit(solution)/shard_map/all_gather | solution.py:137
  494.8 20.2 %all-gather.29.cloned.1.call-done = bf16[2,512,768]{2,1,0:T(8,128)(2,1)} async-done(((bf16[2,128,768]{2,1,0:T(8,128)(2,1)}), bf16[2,512,768]{2,1,0:T(8,128)(2,1)}) %all-gather.29.cloned.1.call-update) | async-done | bytes 1572880 | tf_op jit(solution)/shard_map/all_gather | solution.py:33
  515.0 6.8 fusion.220
  523.0 2.6 convolution_convert_fusion.3
  525.7 28.2 %reduce-scatter.41.cloned.1.call-done = bf16[2,128,768]{2,1,0:T(8,128)(2,1)} async-done(((bf16[2,512,768]{2,1,0:T(8,128)(2,1)}), bf16[2,128,768]{2,1,0:T(8,128)(2,1)}) %reduce-scatter.41.cloned.1.call-update) | async-done | bytes 393232 | tf_op jit(solution)/shard_map/reduce_scatter | solution.py:37
  560.8 19.8 %all-gather.31.cloned.1.call-done = bf16[2,512,768]{2,1,0:T(8,128)(2,1)} async-done(((bf16[2,128,768]{2,1,0:T(8,128)(2,1)}), bf16[2,512,768]{2,1,0:T(8,128)(2,1)}) %all-gather.31.cloned.1.call-update) | async-done | bytes 1572880 | tf_op jit(solution)/shard_map/all_gather | solution.py:33
  586.7 56.8 %while.58 = (s32[]{:T(128)}, bf16[6,512,64]{1,2,0:T(8,128)(2,1)S(1)}, f32[6,1024,64]{1,2,0:T(8,128)}, f32[6,1024,64]{1,2,0:T(8,128)}, s32[6,1024]{1,0:T(8,128)S(...) while((s32[]{:T(128)}, ...), condition=%wide.region_25.26_spmd.clone, body=%wide.region_23.25_spmd.clone.sunk | while | flops 342982144 | bytes 17733776 | solution.py:359
  649.0 9.9 collective-permute-done.5
  659.0 7.6 collective-permute-done.6
  669.4 2.7 bitcast_convert_fusion.1
  672.2 27.3 %reduce-scatter.43.cloned.1.call-done = bf16[2,128,768]{2,1,0:T(8,128)(2,1)} async-done(((bf16[2,512,768]{2,1,0:T(8,128)(2,1)}), bf16[2,128,768]{2,1,0:T(8,128)(2,1)}) %reduce-scatter.43.cloned.1.call-update) | async-done | bytes 393232 | tf_op jit(solution)/shard_map/reduce_scatter | solution.py:37
  706.1 19.8 %all-gather.33.cloned.1.call-done = bf16[2,512,768]{2,1,0:T(8,128)(2,1)} async-done(((bf16[2,128,768]{2,1,0:T(8,128)(2,1)}), bf16[2,512,768]{2,1,0:T(8,128)(2,1)}) %all-gather.33.cloned.1.call-update) | async-done | bytes 1572880 | tf_op jit(solution)/shard_map/all_gather | solution.py:33
  725.9 6.8 fusion.219
  736.6 28.2 %reduce-scatter.45.cloned.1.call-done = bf16[2,128,768]{2,1,0:T(8,128)(2,1)} async-done(((bf16[2,512,768]{2,1,0:T(8,128)(2,1)}), bf16[2,128,768]{2,1,0:T(8,128)(2,1)}) %reduce-scatter.45.cloned.1.call-update) | async-done | bytes 393232 | tf_op jit(solution)/shard_map/reduce_scatter | solution.py:37
  773.8 16.6 %all-gather.35.cloned.1.call-done = bf16[2,512,768]{2,1,0:T(8,128)(2,1)} async-done(((bf16[2,128,768]{2,1,0:T(8,128)(2,1)}), bf16[2,512,768]{2,1,0:T(8,128)(2,1)}) %all-gather.35.cloned.1.call-update) | async-done | bytes 1572880 | tf_op jit(solution)/shard_map/all_gather | solution.py:33
  793.3 4.4 bitcast_convert_fusion.5
  798.0 5.3 bitcast_convert_fusion.4
  803.5 3.9 bitcast_convert_fusion.2
  807.4 5.2 bitcast_convert_fusion.6
  812.7 4.5 bitcast_convert_fusion.7
  822.5 69.3 %while.59 = (s32[]{:T(128)}, bf16[6,512,64]{1,2,0:T(8,128)(2,1)}, f32[6,1024,64]{1,2,0:T(8,128)}, f32[6,1024,64]{1,2,0:T(8,128)S(1)}, s32[6,1024]{1,0:T(8,128)},...) while((s32[]{:T(128)}, bf16[6,512,64]{1,2,0:T(8,128)(2,1)}, ...), condition=%wide.region_34.35_spmd.clone, body=%wide.region_32.34_spmd.clone.sunk | while | flops 342982144 | bytes 17733776 | solution.py:359
  896.2 10.9 collective-permute-done.7
  907.2 7.6 collective-permute-done.8
  916.5 3.5 bitcast_convert_fusion.3
  931.4 4.5 bitcast_convert_fusion
  936.0 5.2 convolution_convert_fusion.4
  944.6 10.2 reduce-scatter.53.cloned.1.call-done
  954.8 30.2 %reduce-scatter.51.cloned.1.call-done = bf16[192,768]{1,0:T(8,128)(2,1)} async-done(((bf16[768,768]{1,0:T(8,128)(2,1)}), bf16[192,768]{1,0:T(8,128)(2,1)}) %reduce-scatter.51.cloned.1.call-update) | async-done | bytes 294928 | tf_op jit(solution)/shard_map/reduce_scatter | solution.py:283
  985.0 30.1 %reduce-scatter.49.cloned.1.call-done = bf16[192,3,192]{2,0,1:T(8,128)(2,1)} async-done(((bf16[768,3,192]{2,0,1:T(8,128)(2,1)}), bf16[192,3,192]{2,0,1:T(8,128)(2,1)}) %reduce-scatter.49.cloned.1.call-update) | async-done | bytes 221200 | tf_op jit(solution)/shard_map/reduce_scatter | solution.py:265
  1016.1 19.3 %reduce-scatter.71.cloned.1.call-done = bf16[16,12]{1,0:T(8,128)(2,1)} async-done(((bf16[64,12]{1,0:T(8,128)(2,1)}), bf16[16,12]{1,0:T(8,128)(2,1)}) %reduce-scatter.71.cloned.1.call-update) | async-done | bytes 400
  1036.1 19.2 %reduce-scatter.67.cloned.1.call-done = bf16[16,6]{1,0:T(8,128)(2,1)} async-done(((bf16[64,6]{1,0:T(8,128)(2,1)}), bf16[16,6]{1,0:T(8,128)(2,1)}) %reduce-scatter.67.cloned.1.call-update) | async-done | bytes 208
  1056.2 18.9 %reduce-scatter.65.cloned.1.call-done = bf16[16,12]{1,0:T(8,128)(2,1)} async-done(((bf16[64,12]{1,0:T(8,128)(2,1)}), bf16[16,12]{1,0:T(8,128)(2,1)}) %reduce-scatter.65.cloned.1.call-update) | async-done | bytes 400
  1075.9 19.1 %reduce-scatter.61.cloned.1.call-done = bf16[16,6]{1,0:T(8,128)(2,1)} async-done(((bf16[64,6]{1,0:T(8,128)(2,1)}), bf16[16,6]{1,0:T(8,128)(2,1)}) %reduce-scatter.61.cloned.1.call-update) | async-done | bytes 208
  1095.8 27.8 %reduce-scatter.47.cloned.1.call-done = bf16[2,128,768]{2,1,0:T(8,128)(2,1)} async-done(((bf16[2,512,768]{2,1,0:T(8,128)(2,1)}), bf16[2,128,768]{2,1,0:T(8,128)(2,1)}) %reduce-scatter.47.cloned.1.call-update) | async-done | bytes 393232 | tf_op jit(solution)/shard_map/reduce_scatter | solution.py:37
  1126.6 10.6 all-reduce.24
  1137.2 19.2 %all-reduce.25 = (bf16[768]{0:T(1024)(128)(2,1)S(1)}, bf16[768]{0:T(1024)(128)(2,1)S(1)}, bf16[768]{0:T(1024)(128)(2,1)S(1)}, bf16[768]{0:T(1024)(128)(2,1)S(1)}...) all-reduce(bf16[768]{0:T(1024)(128)(2,1)S(1)} %dynamic-update-slice, ...), channel_id=1, replica_groups=mesh['dp'=4,'ctx'=2,'tp'=4] {'dp'}, use_global_device_ids=true, to_apply=%add.11 | all-reduce | flops 9984 | bytes 39936
  1157.3 8.3 all-reduce.27
  (699 shorter events, 336.1 us)
Async XLA Ops:
  8.1 41.5 %copy-start.40 = (bf16[192,192]{1,0:T(8,128)(2,1)S(1)}, bf16[192,192]{1,0:T(8,128)(2,1)}, u32[]{:S(2)}) copy-start(bf16[192,192]{1,0:T(8,128)(2,1)} %param.42) | copy-start | bytes 221188
  8.1 94.8 %all-gather.13.cloned.1.call-start = ((), (), s32[]{:S(2)}) async-start(), calls=%async_computation.20 | async-start | bytes 1966080 | tf_op jit(solution)/shard_map/all_gather | solution.py:33
  45.7 129.3 %reduce-scatter.33.cloned.1.call-start = ((), (), s32[]{:S(2)}) async-start(), calls=%async_computation.21 | async-start | bytes 1966080 | tf_op jit(solution)/shard_map/reduce_scatter | solution.py:37
  45.7 57.1 %collective-permute-start = (s32[2,512]{1,0:T(2,128)S(1)}, s32[2,512]{1,0:T(2,128)S(1)}, u32[]{:S(2)}, u32[]{:S(2)}) collective-permute-start(s32[2,512]{1,0:T(2,128)S(1)} %copy-done.61), channel_id=1, source_target_pairs={{0,4},{1,5},{2,6},{3,7},{8,12},{9,13},{10,14},{11,15},{16,20},{17,... | collective-permute-start | bytes 12296 | tf_op jit(solution)/shard_map/ppermute | solution.py:17
  101.6 41.5 %copy-start.11 = (bf16[192,768]{0,1:T(8,128)(2,1)}, bf16[192,768]{0,1:T(8,128)(2,1)S(1)}, u32[]{:S(2)}) copy-start(bf16[192,768]{0,1:T(8,128)(2,1)S(1)} %all_gather.101) | copy-start | bytes 884740
  105.6 6.6 collective-permute-start.2
  107.0 9.5 collective-permute-start.1
  144.9 48.9 %all-gather.17.cloned.1.call-start = ((), (), s32[]{:S(2)}) async-start(), calls=%async_computation.23 | async-start | bytes 1474560 | tf_op jit(solution)/shard_map/all_gather | solution.py:135
  145.5 54.3 %all-gather.15.cloned.1.call-start = ((), (), s32[]{:S(2)}) async-start(), calls=%async_computation.22 | async-start | bytes 1966080 | tf_op jit(solution)/shard_map/all_gather | solution.py:33
  179.5 52.1 %all-gather.19.cloned.1.call-start = ((), (), s32[]{:S(2)}) async-start(), calls=%async_computation.24 | async-start | bytes 1474560 | tf_op jit(solution)/shard_map/all_gather | solution.py:137
  180.1 84.5 %reduce-scatter.35.cloned.1.call-start = ((), (), s32[]{:S(2)}) async-start(), calls=%async_computation.25 | async-start | bytes 1966080 | tf_op jit(solution)/shard_map/reduce_scatter | solution.py:37
  204.6 60.0 %copy-start.1 = (bf16[2,128,768]{2,1,0:T(8,128)(2,1)S(1)}, bf16[2,128,768]{2,1,0:T(8,128)(2,1)}, u32[]{:S(2)}) copy-start(bf16[2,128,768]{2,1,0:T(8,128)(2,1)} %reduce-scatter.33.cloned.1.call-done) | copy-start | bytes 1179652
  237.1 92.2 %all-gather.21.cloned.1.call-start = ((), (), s32[]{:S(2)}) async-start(), calls=%async_computation.26 | async-start | bytes 1966080 | tf_op jit(solution)/shard_map/all_gather | solution.py:33
  267.1 143.1 %reduce-scatter.37.cloned.1.call-start = ((), (), s32[]{:S(2)}) async-start(), calls=%async_computation.27 | async-start | bytes 1966080 | tf_op jit(solution)/shard_map/reduce_scatter | solution.py:37
  267.5 45.8 %copy-start.41 = (bf16[192,192]{1,0:T(8,128)(2,1)S(1)}, bf16[192,192]{1,0:T(8,128)(2,1)}, u32[]{:S(2)}) copy-start(bf16[192,192]{1,0:T(8,128)(2,1)} %param.54) | copy-start | bytes 221188
  332.2 9.5 collective-permute-start.4
  335.7 10.3 collective-permute-start.3
  379.9 62.3 %all-gather.25.cloned.1.call-start = ((), (), s32[]{:S(2)}) async-start(), calls=%async_computation.29 | async-start | bytes 1474560 | tf_op jit(solution)/shard_map/all_gather | solution.py:135
  380.7 82.4 %all-gather.23.cloned.1.call-start = ((), (), s32[]{:S(2)}) async-start(), calls=%async_computation.28 | async-start | bytes 1966080 | tf_op jit(solution)/shard_map/all_gather | solution.py:33
  412.6 82.2 %all-gather.27.cloned.1.call-start = ((), (), s32[]{:S(2)}) async-start(), calls=%async_computation.30 | async-start | bytes 1474560 | tf_op jit(solution)/shard_map/all_gather | solution.py:137
  413.2 101.8 %all-gather.29.cloned.1.call-start = ((), (), s32[]{:S(2)}) async-start(), calls=%async_computation.32 | async-start | bytes 1966080 | tf_op jit(solution)/shard_map/all_gather | solution.py:33
  413.8 140.1 %reduce-scatter.41.cloned.1.call-start = ((), (), s32[]{:S(2)}) async-start(), calls=%async_computation.33 | async-start | bytes 1966080 | tf_op jit(solution)/shard_map/reduce_scatter | solution.py:37
  427.7 87.3 %copy-start.77 = (f32[768]{0:T(1024)}, f32[768]{0:T(1024)S(1)}, u32[]{:S(2)}) copy-start(f32[768]{0:T(1024)S(1)} %reshape.404) | copy-start | bytes 9220
  467.8 55.2 %copy-start.89 = (bf16[768,768]{1,0:T(8,128)(2,1)S(1)}, bf16[768,768]{1,0:T(8,128)(2,1)}, u32[]{:S(2)}) copy-start(bf16[768,768]{1,0:T(8,128)(2,1)} %all-gather.25.cloned.1.call-done) | copy-start | bytes 3538948
  525.6 54.9 %all-gather.31.cloned.1.call-start = ((), (), s32[]{:S(2)}) async-start(), calls=%async_computation.34 | async-start | bytes 1966080 | tf_op jit(solution)/shard_map/all_gather | solution.py:33
  560.7 138.8 %reduce-scatter.43.cloned.1.call-start = ((), (), s32[]{:S(2)}) async-start(), calls=%async_computation.35 | async-start | bytes 1966080 | tf_op jit(solution)/shard_map/reduce_scatter | solution.py:37
  644.9 14.0 %collective-permute-start.5 = (bf16[2,512,192]{1,2,0:T(8,128)(2,1)S(1)}, bf16[2,512,192]{1,2,0:T(8,128)(2,1)S(1)}, u32[]{:S(2)}, u32[]{:S(2)}) collective-permute-start(bf16[2,512,192]{1,2,0:T(8,128)(2,1)S(1)} %slice.333), channel_id=1, source_target_pairs={{4,0},{5,1},{6,2},{7,3},{12,8},{13,9},{14,10},{15,11},{20,16},{21,... | collective-permute-start | bytes 1179656 | tf_op jit(solution)/shard_map/ppermute | solution.py:17
  647.5 19.1 %collective-permute-start.6 = (bf16[2,512,192]{1,2,0:T(8,128)(2,1)S(1)}, bf16[2,512,192]{1,2,0:T(8,128)(2,1)S(1)}, u32[]{:S(2)}, u32[]{:S(2)}) collective-permute-start(bf16[2,512,192]{1,2,0:T(8,128)(2,1)S(1)} %slice.332), channel_id=1, source_target_pairs={{4,0},{5,1},{6,2},{7,3},{12,8},{13,9},{14,10},{15,11},{20,16},{21,... | collective-permute-start | bytes 1179656 | tf_op jit(solution)/shard_map/ppermute | solution.py:17
  672.1 53.8 %all-gather.33.cloned.1.call-start = ((), (), s32[]{:S(2)}) async-start(), calls=%async_computation.36 | async-start | bytes 1966080 | tf_op jit(solution)/shard_map/all_gather | solution.py:33
  706.1 58.7 %reduce-scatter.45.cloned.1.call-start = ((), (), s32[]{:S(2)}) async-start(), calls=%async_computation.37 | async-start | bytes 1966080 | tf_op jit(solution)/shard_map/reduce_scatter | solution.py:37
  736.5 53.9 %all-gather.35.cloned.1.call-start = ((), (), s32[]{:S(2)}) async-start(), calls=%async_computation.38 | async-start | bytes 1966080 | tf_op jit(solution)/shard_map/all_gather | solution.py:33
  770.8 170.6 %reduce-scatter.69.cloned.1.call-start = ((), (), s32[]{:S(2)}) async-start(), calls=%async_computation.50 | async-start | bytes 491520
  773.7 169.3 %reduce-scatter.63.cloned.1.call-start = ((), (), s32[]{:S(2)}) async-start(), calls=%async_computation.47 | async-start | bytes 491520
  793.2 151.4 %reduce-scatter.57.cloned.1.call-start = ((), (), s32[]{:S(2)}) async-start(), calls=%async_computation.44 | async-start | bytes 1474560 | tf_op jit(solution)/shard_map/reduce_scatter | solution.py:283
  797.8 146.9 %reduce-scatter.59.cloned.1.call-start = ((), (), s32[]{:S(2)}) async-start(), calls=%async_computation.45 | async-start | bytes 1474560 | tf_op jit(solution)/shard_map/reduce_scatter | solution.py:289
  803.4 141.3 %reduce-scatter.55.cloned.1.call-start = ((), (), s32[]{:S(2)}) async-start(), calls=%async_computation.43 | async-start | bytes 1474560 | tf_op jit(solution)/shard_map/reduce_scatter | solution.py:265
  807.3 147.4 %reduce-scatter.53.cloned.1.call-start = ((), (), s32[]{:S(2)}) async-start(), calls=%async_computation.42 | async-start | bytes 1474560 | tf_op jit(solution)/shard_map/reduce_scatter | solution.py:289
  812.7 172.3 %reduce-scatter.51.cloned.1.call-start = ((), (), s32[]{:S(2)}) async-start(), calls=%async_computation.41 | async-start | bytes 1474560 | tf_op jit(solution)/shard_map/reduce_scatter | solution.py:283
  817.2 197.9 %reduce-scatter.49.cloned.1.call-start = ((), (), s32[]{:S(2)}) async-start(), calls=%async_computation.40 | async-start | bytes 1474560 | tf_op jit(solution)/shard_map/reduce_scatter | solution.py:265
  893.1 14.0 %collective-permute-start.7 = (bf16[2,512,192]{1,2,0:T(8,128)(2,1)S(1)}, bf16[2,512,192]{1,2,0:T(8,128)(2,1)S(1)}, u32[]{:S(2)}, u32[]{:S(2)}) collective-permute-start(bf16[2,512,192]{1,2,0:T(8,128)(2,1)S(1)} %slice.331), channel_id=1, source_target_pairs={{4,0},{5,1},{6,2},{7,3},{12,8},{13,9},{14,10},{15,11},{20,16},{21,... | collective-permute-start | bytes 1179656 | tf_op jit(solution)/shard_map/ppermute | solution.py:17
  894.6 20.2 %collective-permute-start.8 = (bf16[2,512,192]{1,2,0:T(8,128)(2,1)S(1)}, bf16[2,512,192]{1,2,0:T(8,128)(2,1)S(1)}, u32[]{:S(2)}, u32[]{:S(2)}) collective-permute-start(bf16[2,512,192]{1,2,0:T(8,128)(2,1)S(1)} %slice.330), channel_id=1, source_target_pairs={{4,0},{5,1},{6,2},{7,3},{12,8},{13,9},{14,10},{15,11},{20,16},{21,... | collective-permute-start | bytes 1179656 | tf_op jit(solution)/shard_map/ppermute | solution.py:17
  920.1 115.3 %reduce-scatter.71.cloned.1.call-start = ((), (), s32[]{:S(2)}) async-start(), calls=%async_computation.51 | async-start | bytes 20480
  920.9 134.4 %reduce-scatter.67.cloned.1.call-start = ((), (), s32[]{:S(2)}) async-start(), calls=%async_computation.49 | async-start | bytes 20480
  927.1 148.0 %reduce-scatter.65.cloned.1.call-start = ((), (), s32[]{:S(2)}) async-start(), calls=%async_computation.48 | async-start | bytes 20480
  928.0 166.9 %reduce-scatter.61.cloned.1.call-start = ((), (), s32[]{:S(2)}) async-start(), calls=%async_computation.46 | async-start | bytes 20480
  931.3 192.3 %reduce-scatter.47.cloned.1.call-start = ((), (), s32[]{:S(2)}) async-start(), calls=%async_computation.39 | async-start | bytes 1966080 | tf_op jit(solution)/shard_map/reduce_scatter | solution.py:37
  935.9 238.9 %reduce-scatter.39.cloned.1.call-start = ((), (), s32[]{:S(2)}) async-start(), calls=%async_computation.31 | async-start | bytes 1966080 | tf_op jit(solution)/shard_map/reduce_scatter | solution.py:37
  941.1 74.0 %copy-start.90 = (bf16[192]{0:T(256)(128)(2,1)S(1)}, bf16[192]{0:T(256)(128)(2,1)}, u32[]{:S(2)}) copy-start(bf16[192]{0:T(256)(128)(2,1)} %param.61) | copy-start | bytes 1156
  941.1 182.5 %copy-start.39 = (f32[768]{0:T(1024)S(1)}, f32[768]{0:T(1024)}, u32[]{:S(2)}) copy-start(f32[768]{0:T(1024)} %copy-done.38) | copy-start | bytes 9220
  941.1 182.5 %copy-start.46 = (f32[2,128]{1,0:T(2,128)S(1)}, f32[2,128]{1,0:T(2,128)}, u32[]{:S(2)}) copy-start(f32[2,128]{1,0:T(2,128)} %copy-done.45) | copy-start | bytes 3076
  941.1 183.9 %copy-start.63 = (f32[2,128]{1,0:T(2,128)S(1)}, f32[2,128]{1,0:T(2,128)}, u32[]{:S(2)}) copy-start(f32[2,128]{1,0:T(2,128)} %copy-done.62) | copy-start | bytes 3076
  941.1 183.9 %copy-start.48 = (f32[2,128]{1,0:T(2,128)S(1)}, f32[2,128]{1,0:T(2,128)}, u32[]{:S(2)}) copy-start(f32[2,128]{1,0:T(2,128)} %copy-done.47) | copy-start | bytes 3076
  941.2 185.4 %copy-start.51 = (f32[768]{0:T(1024)S(1)}, f32[768]{0:T(1024)}, u32[]{:S(2)}) copy-start(f32[768]{0:T(1024)} %get-tuple-element.664) | copy-start | bytes 9220
  941.2 185.4 %copy-start.52 = (f32[768]{0:T(1024)S(1)}, f32[768]{0:T(1024)}, u32[]{:S(2)}) copy-start(f32[768]{0:T(1024)} %get-tuple-element.658) | copy-start | bytes 9220
  941.2 185.4 %copy-start.53 = (f32[768]{0:T(1024)S(1)}, f32[768]{0:T(1024)}, u32[]{:S(2)}) copy-start(f32[768]{0:T(1024)} %get-tuple-element.824) | copy-start | bytes 9220
  941.2 185.4 %copy-start.54 = (f32[768]{0:T(1024)S(1)}, f32[768]{0:T(1024)}, u32[]{:S(2)}) copy-start(f32[768]{0:T(1024)} %get-tuple-element.854) | copy-start | bytes 9220
  941.2 185.4 %copy-start.55 = (f32[768]{0:T(1024)S(1)}, f32[768]{0:T(1024)}, u32[]{:S(2)}) copy-start(f32[768]{0:T(1024)} %get-tuple-element.666) | copy-start | bytes 9220
  941.2 185.4 %copy-start.56 = (f32[768]{0:T(1024)S(1)}, f32[768]{0:T(1024)}, u32[]{:S(2)}) copy-start(f32[768]{0:T(1024)} %get-tuple-element.660) | copy-start | bytes 9220
  941.2 185.4 %copy-start.57 = (f32[768]{0:T(1024)S(1)}, f32[768]{0:T(1024)}, u32[]{:S(2)}) copy-start(f32[768]{0:T(1024)} %get-tuple-element.826) | copy-start | bytes 9220
  941.2 185.4 %copy-start.58 = (f32[768]{0:T(1024)S(1)}, f32[768]{0:T(1024)}, u32[]{:S(2)}) copy-start(f32[768]{0:T(1024)} %get-tuple-element.668) | copy-start | bytes 9220
  941.2 185.4 %copy-start.59 = (f32[768]{0:T(1024)S(1)}, f32[768]{0:T(1024)}, u32[]{:S(2)}) copy-start(f32[768]{0:T(1024)} %get-tuple-element.656) | copy-start | bytes 9220
  941.3 185.4 %copy-start.60 = (f32[768]{0:T(1024)S(1)}, f32[768]{0:T(1024)}, u32[]{:S(2)}) copy-start(f32[768]{0:T(1024)} %get-tuple-element.828) | copy-start | bytes 9220
  941.3 236.5 %all-reduce.31.cloned.1.call-start = ((), (), s32[]{:S(2)}) async-start(), calls=%async_computation.52 | async-start | bytes 3932160 | tf_op jit(solution)/shard_map/psum | solution.py:233
  1123.6 53.0 %copy-start.12 = (bf16[2,128,768]{2,1,0:T(8,128)(2,1)S(1)}, bf16[2,128,768]{2,1,0:T(8,128)(2,1)}, u32[]{:S(2)}) copy-start(bf16[2,128,768]{2,1,0:T(8,128)(2,1)} %reduce-scatter.47.cloned.1.call-done) | copy-start | bytes 1179652
  (75 other events, 1061.1 us)
Sparse Core Ops, SparseCore 0:
  45.8 17.8 all-gather.12
  145.0 29.9 reduce-scatter.32
  237.2 27.3 reduce-scatter.34
  525.8 28.1 reduce-scatter.40
  560.8 19.6 all-gather.30
  672.2 27.2 reduce-scatter.42
  706.2 19.6 all-gather.32
  736.7 28.1 reduce-scatter.44
  1015.3 59.8 all-reduce.30
Sparse Core Ops, SparseCore 1:
  147.0 31.9 all-gather.16
  181.1 18.7 all-gather.14
  201.3 30.2 all-gather.18
  267.2 19.5 all-gather.20
  380.0 30.1 reduce-scatter.36
  411.9 30.3 all-gather.24
  444.3 18.6 all-gather.22
  464.5 30.2 all-gather.26
  496.3 18.7 all-gather.28
  770.9 19.5 all-gather.34
  792.6 20.6 reduce-scatter.68
  816.2 18.6 reduce-scatter.62
  837.0 27.2 reduce-scatter.56
  866.6 27.8 reduce-scatter.58
  896.8 27.8 reduce-scatter.54
  926.9 27.8 reduce-scatter.52
  957.1 27.8 reduce-scatter.50
  987.3 27.8 reduce-scatter.48
  1017.8 17.5 reduce-scatter.70
  1038.3 17.0 reduce-scatter.66
  1058.0 17.0 reduce-scatter.64
  1077.9 17.0 reduce-scatter.60
  1097.3 26.2 reduce-scatter.46
  1126.4 28.1 reduce-scatter.38
where the time goes:
time: 1210 us; the launch traced here: 1190 us
  waiting for transfers between devices  566 us (47%)
  matrix products  246 us (20%)
  blocking collectives  197 us (16%)
  local copies, waits for them, and re-layouts  75.1 us (6%)
  other arithmetic  73.2 us (6%)
  between operations  19 us (2%)
  starting transfers between devices  18.3 us (2%)
    reduce_scatter x8, waiting for transfers between devices, gather_sums(): lax.psum_scatter(partial_value.astype(jnp.bfloat16), 'tp', scatter_dimens...  198 us
    all_gather x8, waiting for transfers between devices, spread_rows(): return lax.all_gather(row_block, 'tp', axis=1, tiled=True)  103 us
    unnamed x39, waiting for transfers between devices  79.8 us
    all_gather x2, blocking collectives, layer_forward(): lax.all_gather(merged_weight, 'dp', axis=0, tiled=True)  54.2 us
    all_gather x2, waiting for transfers between devices, layer_forward(): lax.all_gather(reduce_weight, 'dp', axis=1, tiled=True)  53.9 us
    dot_general x24, matrix products, masked_scores(): jnp.einsum('qd,kd->qk', query_rows, key_rows, preferred_element_type=jnp....  51.8 us
    ppermute x9, waiting for transfers between devices, from_behind(): return lax.ppermute(block, axis, route)  45.7 us
    unnamed x265, local copies, waits for them, and re-layouts  45.6 us
  transfers between devices with their start and end apart: 42, of which 31 were waited for; matrix products, arithmetic and copies ran while one was open for 15% of the time, Pallas kernels for 0%

commit v1 on v0

--- a/solution.py
+++ b/solution.py
@@ -1,6 +1,8 @@
 import jax
 import jax.numpy as jnp
 from jax import lax
+from jax.experimental import pallas as pl
+from jax.experimental.pallas import tpu as pltpu
 from jax.sharding import PartitionSpec as P
 
 HD = 64
@@ -434,7 +436,7 @@
     return (grad_input, reduce_grads(fresh))
 
 
-def shards(
+def general_shards(
     inputs,
     segments,
     cotangent,
@@ -527,7 +529,594 @@
     )
 
 
+BF16 = jnp.bfloat16
+F32 = jnp.float32
+NEG = -1e30
+TILE = 256
+RELATIVE = (0, 2, 1, 3)
+
+
+def swap(value, axis, bit):
+    route = [(i, i ^ bit) for i in range(lax.axis_size(axis))]
+    return lax.ppermute(value, axis, route)
+
+
+def cross_core(value):
+    return swap(value, "tp", 1)
+
+
+def cross_x(value):
+    return swap(value, "tp", 2)
+
+
+def cross_y(value):
+    return swap(value, "ctx", 1)
+
+
+def shift_z(value, distance):
+    count = lax.axis_size("dp")
+    return lax.ppermute(value, "dp", [(i, (i + distance) % count) for i in range(count)])
+
+
+def gather_z(piece):
+    return [piece] + [shift_z(piece, k) for k in range(1, lax.axis_size("dp"))]
+
+
+def scatter_z(pieces):
+    total = pieces[0].astype(F32)
+    for k in range(1, len(pieces)):
+        total = total + shift_z(pieces[k].astype(BF16), -k).astype(F32)
+    return total
+
+
+def y_order(own, other, y_index, axis):
+    return jnp.where(
+        y_index == 0,
+        jnp.concatenate([own, other], axis=axis),
+        jnp.concatenate([other, own], axis=axis),
+    )
+
+
+def window_start(block, doc_max):
+    return max(0, (block * TILE - doc_max + 1) // TILE) * TILE
+
+
+def load_rows(source, target, me, columns, scale=None):
+    rows = source.shape[0] // 8
+    for r in range(4):
+        for half in range(2):
+            place = pl.multiple_of((half * 4 + (me ^ RELATIVE[r])) * rows, rows)
+            value = source[(r * 2 + half) * rows : (r * 2 + half + 1) * rows, columns]
+            if scale is not None:
+                value = value * scale
+            target[pl.ds(place, rows), columns] = value
+
+
+def store_rows(source, target, me):
+    rows = target.shape[0] // 8
+    for r in range(4):
+        for half in range(2):
+            place = pl.multiple_of((half * 4 + (me ^ RELATIVE[r])) * rows, rows)
+            target[(r * 2 + half) * rows : (r * 2 + half + 1) * rows, :] = source[
+                pl.ds(place, rows), :
+            ].astype(target.dtype)
+
+
+def keep_mask(row_docs, column_docs, block, start):
+    size = (block + 1) * TILE - start
+    rows = block * TILE + lax.broadcasted_iota(jnp.int32, (TILE, size), 0)
+    columns = start + lax.broadcasted_iota(jnp.int32, (TILE, size), 1)
+    same = (
+        row_docs[block * TILE : (block + 1) * TILE, :] == column_docs[:, start : start + size]
+    )
+    return same & (columns <= rows)
+
+
+def attention_forward_kernel(
+    heads, doc_max, me_ref, qkv_ref, row_docs, column_docs, mixed_ref, log_ref, qkv, mixed
+):
+    me = me_ref[0]
+    width = heads * HD
+    load_rows(qkv_ref, qkv, me, slice(0, width), BF16(0.125))
+    load_rows(qkv_ref, qkv, me, slice(width, 3 * width))
+    for block in range(qkv.shape[0] // TILE):
+        start = window_start(block, doc_max)
+        stop = (block + 1) * TILE
+        mask = keep_mask(row_docs, column_docs, block, start)
+        here = slice(block * TILE, stop)
+        for h in range(heads):
+            at = slice(h * HD, (h + 1) * HD)
+            query = qkv[here, at]
+            key = qkv[start:stop, width + h * HD : width + (h + 1) * HD]
+            value = qkv[start:stop, 2 * width + h * HD : 2 * width + (h + 1) * HD]
+            scores = lax.dot_general(
+                query, key, (((1,), (1,)), ((), ())), preferred_element_type=F32
+            )
+            scores = jnp.where(mask, scores, NEG)
+            top = jnp.max(scores, axis=-1, keepdims=True)
+            raised = jnp.exp(scores - top)
+            total = jnp.sum(raised, axis=-1, keepdims=True)
+            weights = (raised * (1.0 / total)).astype(BF16)
+            mixed[here, at] = jnp.dot(weights, value, preferred_element_type=F32).astype(BF16)
+            log_ref[here, h : h + 1] = top + jnp.log(total)
+    store_rows(mixed, mixed_ref, me)
+
+
+def attention_backward_kernel(
+    heads,
+    doc_max,
+    me_ref,
+    qkv_ref,
+    row_docs,
+    column_docs,
+    log_ref,
+    mixed_ref,
+    grad_ref,
+    out_ref,
+    qkv,
+    grad,
+    mixed,
+    total,
+):
+    me = me_ref[0]
+    width = heads * HD
+    load_rows(qkv_ref, qkv, me, slice(0, width), BF16(0.125))
+    load_rows(qkv_ref, qkv, me, slice(width, 3 * width))
+    load_rows(grad_ref, grad, me, slice(0, width))
+    load_rows(mixed_ref, mixed, me, slice(0, width))
+    total[:, width:] = jnp.zeros((total.shape[0], 2 * width), F32)
+    for block in range(qkv.shape[0] // TILE):
+        start = window_start(block, doc_max)
+        stop = (block + 1) * TILE
+        mask = keep_mask(row_docs, column_docs, block, start)
+        here = slice(block * TILE, stop)
+        for h in range(heads):
+            at = slice(h * HD, (h + 1) * HD)
+            at_key = slice(width + h * HD, width + (h + 1) * HD)
+            at_value = slice(2 * width + h * HD, 2 * width + (h + 1) * HD)
+            query = qkv[here, at]
+            key = qkv[start:stop, at_key]
+            value = qkv[start:stop, at_value]
+            grad_rows = grad[here, at]
+            scores = lax.dot_general(
+                query, key, (((1,), (1,)), ((), ())), preferred_element_type=F32
+            )
+            weights = jnp.where(mask, jnp.exp(scores - log_ref[here, h : h + 1]), 0.0)
+            grad_weights = lax.dot_general(
+                grad_rows, value, (((1,), (1,)), ((), ())), preferred_element_type=F32
+            )
+            centered = jnp.sum(
+                grad_rows.astype(F32) * mixed[here, at].astype(F32), axis=-1, keepdims=True
+            )
+            grad_scores = (weights * (grad_weights - centered)).astype(BF16)
+            total[here, at] = jnp.dot(grad_scores, key, preferred_element_type=F32) * 0.125
+            total[start:stop, at_key] += lax.dot_general(
+                grad_scores, query, (((0,), (0,)), ((), ())), preferred_element_type=F32
+            )
+            total[start:stop, at_value] += lax.dot_general(
+                weights.astype(BF16), grad_rows, (((0,), (0,)), ((), ())), preferred_element_type=F32
+            )
+    store_rows(total, out_ref, me)
+
+
+def attention_forward(qkv, me, row_docs, column_docs, doc_max):
+    length, width = qkv.shape[0], qkv.shape[1] // 3
+    heads = width // HD
+    area = heads * length * length // 2
+    vmem = pl.BlockSpec(memory_space=pltpu.VMEM)
+
+    def body(*refs):
+        attention_forward_kernel(heads, doc_max, *refs)
+
+    return pl.pallas_call(
+        body,
+        out_shape=(
+            jax.ShapeDtypeStruct((length, width), BF16),
+            jax.ShapeDtypeStruct((length, heads), F32),
+        ),
+        in_specs=[pl.BlockSpec(memory_space=pltpu.SMEM), vmem, vmem, vmem],
+        out_specs=(vmem, vmem),
+        scratch_shapes=[pltpu.VMEM((length, 3 * width), BF16), pltpu.VMEM((length, width), BF16)],
+        cost_estimate=pl.CostEstimate(
+            flops=16 * HD * area, transcendentals=area, bytes_accessed=8 * length * width
+        ),
+        compiler_params=pltpu.CompilerParams(vmem_limit_bytes=40 << 20),
+        name="attention_forward",
+    )(me, qkv, row_docs, column_docs)
+
+
+def attention_backward(qkv, me, row_docs, column_docs, log_total, mixed, grad_mixed, doc_max):
+    length, width = qkv.shape[0], qkv.shape[1] // 3
+    heads = width // HD
+    area = heads * length * length // 2
+    vmem = pl.BlockSpec(memory_space=pltpu.VMEM)
+
+    def body(*refs):
+        attention_backward_kernel(heads, doc_max, *refs)
+
+    return pl.pallas_call(
+        body,
+        out_shape=jax.ShapeDtypeStruct((length, 3 * width), BF16),
+        in_specs=[pl.BlockSpec(memory_space=pltpu.SMEM)] + [vmem] * 6,
+        out_specs=vmem,
+        scratch_shapes=[
+            pltpu.VMEM((length, 3 * width), BF16),
+            pltpu.VMEM((length, width), BF16),
+            pltpu.VMEM((length, width), BF16),
+            pltpu.VMEM((length, 3 * width), F32),
+        ],
+        cost_estimate=pl.CostEstimate(
+            flops=40 * HD * area, transcendentals=area, bytes_accessed=16 * length * width
+        ),
+        compiler_params=pltpu.CompilerParams(vmem_limit_bytes=40 << 20),
+        name="attention_backward",
+    )(me, qkv, row_docs, column_docs, log_total, mixed, grad_mixed)
+
+
+def normalize(values):
+    center = values - jnp.mean(values, axis=-1, keepdims=True)
+    spread = jnp.mean(center * center, axis=-1, keepdims=True)
+    scale = lax.rsqrt(spread + EPSILON)
+    return center * scale, scale
+
+
+def norm_pullback(grad, unit, scale, gain):
+    inner = grad * gain
+    return scale * (
+        inner
+        - jnp.mean(inner, axis=-1, keepdims=True)
+        - unit * jnp.mean(inner * unit, axis=-1, keepdims=True)
+    )
+
+
+def gather_rows(rows):
+    pair = jnp.concatenate([rows, cross_x(rows)], axis=0)
+    return jnp.concatenate([pair, cross_core(pair)], axis=0)
+
+
+def gather_core(rows):
+    return jnp.concatenate([rows, cross_core(rows)], axis=0)
+
+
+def times(left, right, kind=F32):
+    return jnp.dot(left, right, preferred_element_type=F32).astype(kind)
+
+
+def times_across(left, right, kind=F32):
+    return lax.dot_general(
+        left, right, (((1,), (1,)), ((), ())), preferred_element_type=F32
+    ).astype(kind)
+
+
+def times_down(left, right, kind=F32):
+    return lax.dot_general(
+        left, right, (((0,), (0,)), ((), ())), preferred_element_type=F32
+    ).astype(kind)
+
+
+def scatter_rows(left, multiply):
+    half = left.shape[0] // 2
+    quarter = half // 2
+    sent = cross_core(multiply(left[half:], BF16))
+    kept = multiply(left[:half], F32) + sent.astype(F32)
+    return kept[:quarter] + cross_x(kept[quarter:].astype(BF16)).astype(F32)
+
+
+def scatter_core(left, multiply):
+    half = left.shape[0] // 2
+    sent = cross_core(multiply(left[half:], BF16))
+    return multiply(left[:half], F32) + sent.astype(F32)
+
+
+def halves(shard, y_index):
+    middle = shard.shape[0] // 2
+    own = jnp.where(y_index == 0, shard[:middle], shard[middle:])
+    other = jnp.where(y_index == 0, shard[middle:], shard[:middle])
+    return own, other
+
+
+def fetch_matrices(params, y_index):
+    merged, output, expand, reduce = params
+    rows = merged.shape[0]
+    attend_shard = jnp.concatenate([merged.reshape(rows, -1), output.T], axis=1)
+    attend_half, _ = halves(attend_shard, y_index)
+    attend_part = jnp.concatenate(gather_z(attend_half), axis=0)
+    attend = jnp.concatenate([attend_part, cross_y(attend_part)], axis=0)
+    expand_half, _ = halves(expand, y_index)
+    expand_part = jnp.concatenate(gather_z(expand_half), axis=0)
+    expand_part = jnp.concatenate([expand_part, cross_x(expand_part)], axis=1)
+    expand_all = jnp.concatenate([expand_part, cross_y(expand_part)], axis=0)
+    own, other = halves(reduce.T, y_index)
+    pieces = gather_z(jnp.concatenate([own, other], axis=0))
+    middle = rows // 2
+    reduce_part = jnp.concatenate([p[:middle] for p in pieces] + [p[middle:] for p in pieces], axis=0)
+    reduce_all = jnp.concatenate([reduce_part, cross_x(reduce_part)], axis=1)
+    width = merged.shape[2] * 3
+    return attend[:, :width], attend[:, width:], expand_all, reduce_all
+
+
+def finish_y(part, y_index):
+    part = part.astype(BF16)
+    return y_order(part, cross_y(part), y_index, 0).astype(F32)
+
+
+def return_split(grad, y_index):
+    middle = grad.shape[0] // 2
+    return grad[:middle].astype(F32) + cross_y(grad[middle:]).astype(F32)
+
+
+def own_columns(grad):
+    middle = grad.shape[1] // 2
+    return grad[:, :middle].astype(F32) + cross_x(grad[:, middle:].astype(BF16)).astype(F32)
+
+
+def blocks_of(grad, count):
+    rows = grad.shape[0] // count
+    return [grad[k * rows : (k + 1) * rows] for k in range(count)]
+
+
+def return_attend(grad, y_index):
+    count = lax.axis_size("dp")
+    part = return_split(grad, y_index)
+    return finish_y(scatter_z(blocks_of(part, count)), y_index)
+
+
+def return_expand(grad, y_index):
+    count = lax.axis_size("dp")
+    part = own_columns(return_split(grad, y_index))
+    return finish_y(scatter_z(blocks_of(part, count)), y_index)
+
+
+def return_reduce(grad, y_index):
+    count = lax.axis_size("dp")
+    part = blocks_of(own_columns(grad), 2 * count)
+    pieces = [jnp.concatenate([part[k], part[count + k]], axis=0) for k in range(count)]
+    mine = scatter_z(pieces).astype(BF16)
+    middle = mine.shape[0] // 2
+    whole = mine.astype(F32) + cross_y(jnp.concatenate([mine[middle:], mine[:middle]], axis=0)).astype(
+        F32
+    )
+    return jnp.where(y_index == 0, whole, jnp.concatenate([whole[middle:], whole[:middle]], axis=0))
+
+
+def fetch_vectors(blocks, y_index, z_index):
+    count = lax.axis_size("dp")
+    rows = []
+    for block in blocks:
+        gains, merged_bias, expand_bias = block
+        local = gains[0].shape[0]
+        rows.append(jnp.concatenate([g.reshape(1, local) for g in gains], axis=1))
+        rows.append(merged_bias.reshape(1, -1))
+        rows.append(expand_bias.reshape(1, -1))
+    pack = jnp.concatenate(rows, axis=1)
+    pieces = jnp.concatenate(gather_z(pack), axis=0).astype(F32)
+    natural = jnp.take(pieces, (z_index - jnp.arange(count)) % count, axis=0)
+    result = []
+    at = 0
+    for block in blocks:
+        gains, merged_bias, expand_bias = block
+        local = gains[0].shape[0]
+        middle = local // 2
+        part = pieces[:, at : at + 6 * local].reshape(count, 6, 2, middle)
+        part = jnp.where(y_index == 0, part, part[:, :, ::-1])
+        vectors = part.transpose(1, 2, 0, 3).reshape(6, 2 * count * middle)
+        at = at + 6 * local
+        size = merged_bias.size
+        part = natural[:, at : at + size].reshape((count,) + merged_bias.shape)
+        biases = part.transpose(1, 2, 0, 3).reshape(2, -1)
+        at = at + size
+        size = expand_bias.size
+        part = natural[:, at : at + size].reshape((count,) + expand_bias.shape)
+        hidden_bias = part.transpose(1, 0, 2).reshape(1, -1)
+        at = at + size
+        result.append((vectors, biases, hidden_bias))
+    others = cross_x(jnp.concatenate([r[2] for r in result], axis=0).astype(BF16)).astype(F32)
+    return [
+        (r[0], r[1], jnp.concatenate([r[2], others[i : i + 1]], axis=1))
+        for i, r in enumerate(result)
+    ]
+
+
+def fast_forward(stream, weights, vectors, me, row_docs, column_docs, doc_max):
+    merged, output, expand, reduce = weights
+    gains, biases, hidden_bias = vectors
+    width = output.shape[1]
+    unit, scale = normalize(stream)
+    rows = gather_rows((unit * gains[0] + gains[1]).astype(BF16))
+    added = jnp.concatenate([biases[0], jnp.zeros((width,), F32), biases[1]])
+    qkv = (times(rows, merged) + added).astype(BF16)
+    mixed, log_total = attention_forward(qkv, me, row_docs, column_docs, doc_max)
+    middle = stream + gains[2] + scatter_rows(mixed, lambda v, kind: times_across(v, output, kind))
+    unit_two, scale_two = normalize(middle)
+    rows_two = gather_core((unit_two * gains[3] + gains[4]).astype(BF16))
+    hidden = times(rows_two, expand) + hidden_bias
+    active = gelu_tanh(hidden).astype(BF16)
+    result = (
+        middle + gains[5] + scatter_core(active, lambda v, kind: times_across(v, reduce, kind))
+    )
+    saved = (stream, rows, qkv, mixed, log_total, middle, rows_two, hidden, active)
+    return result, saved
+
+
+def fast_backward(grad_out, saved, weights, vectors, me, row_docs, column_docs, doc_max, y_index):
+    stream, rows, qkv, mixed, log_total, middle, rows_two, hidden, active = saved
+    merged, output, expand, reduce = weights
+    gains, biases, hidden_bias = vectors
+    width = output.shape[1]
+    branch = gather_core(grad_out.astype(BF16))
+    grad_reduce = times_down(branch, active, BF16)
+    grad_active = times(branch, reduce)
+    _, gelu_pull = jax.vjp(gelu_tanh, hidden)
+    grad_hidden = gelu_pull(grad_active)[0].astype(BF16)
+    grad_hidden_bias = jnp.sum(grad_hidden.astype(F32), axis=0)
+    grad_expand = times_down(rows_two, grad_hidden, BF16)
+    grad_second = scatter_core(grad_hidden, lambda v, kind: times_across(v, expand, kind))
+    grad_reduce = return_reduce(grad_reduce, y_index)
+    grad_expand = return_expand(grad_expand, y_index)
+    unit_two, scale_two = normalize(middle)
+    grad_middle = grad_out + norm_pullback(grad_second, unit_two, scale_two, gains[3])
+    attend = gather_rows(grad_middle.astype(BF16))
+    grad_mixed = times(attend, output, BF16)
+    grad_qkv = attention_backward(
+        qkv, me, row_docs, column_docs, log_total, mixed, grad_mixed, doc_max
+    )
+    grad_merged = times_down(rows, grad_qkv, BF16)
+    grad_output = times_down(attend, mixed, BF16)
+    grad_pack = return_attend(jnp.concatenate([grad_merged, grad_output], axis=1), y_index)
+    grad_bias = jnp.sum(grad_qkv.astype(F32), axis=0)
+    grad_first = scatter_rows(grad_qkv, lambda v, kind: times_across(v, merged, kind))
+    unit, scale = normalize(stream)
+    grad_in = grad_middle + norm_pullback(grad_first, unit, scale, gains[0])
+    sums = jnp.stack(
+        [
+            jnp.sum(grad_first * unit, axis=0),
+            jnp.sum(grad_first, axis=0),
+            jnp.sum(grad_middle, axis=0),
+            jnp.sum(grad_second * unit_two, axis=0),
+            jnp.sum(grad_second, axis=0),
+            jnp.sum(grad_out, axis=0),
+        ]
+    )
+    biases = jnp.concatenate([grad_bias[:width], grad_bias[2 * width :]])
+    return grad_in, (sums, biases, grad_hidden_bias), (grad_pack, grad_expand, grad_reduce)
+
+
+def return_vectors(grads, shapes, y_index, z_index):
+    count = lax.axis_size("dp")
+    sums = jnp.concatenate([g[0] for g in grads], axis=0)
+    sums = sums + cross_core(sums)
+    sums = sums + cross_x(sums)
+    hidden = jnp.stack([g[2] for g in grads])
+    middle = hidden.shape[1] // 2
+    hidden = hidden[:, :middle] + cross_x(hidden[:, middle:])
+    biases = jnp.stack([g[1] for g in grads])
+    number = len(grads)
+    local = sums.shape[1] // count
+    parts = sums.reshape(6 * number, 2, count, local // 2)
+    parts = jnp.where(y_index == 0, parts, parts[:, ::-1])
+    parts = parts.transpose(2, 0, 1, 3).reshape(count, 1, -1)
+    order = (z_index - jnp.arange(count)) % count
+    bias_parts = jnp.take(
+        biases.reshape(-1, count, biases.shape[1] * number // shapes[0].size * shapes[0].shape[-1])
+        if False
+        else biases.reshape(-1, count, shapes[0].shape[-1]),
+        order,
+        axis=1,
+    )
+    bias_parts = bias_parts.transpose(1, 0, 2).reshape(count, 1, -1)
+    hidden_parts = jnp.take(hidden.reshape(-1, count, shapes[1].shape[-1]), order, axis=1)
+    hidden_parts = hidden_parts.transpose(1, 0, 2).reshape(count, 1, -1)
+    pack = jnp.concatenate([parts, bias_parts, hidden_parts], axis=2)
+    pack = pack + cross_y(pack)
+    total = pack[0]
+    for k in range(1, count):
+        total = total + shift_z(pack[k], -k)
+    result = []
+    first = 6 * number * local
+    bias_size = shapes[0].size
+    hidden_size = shapes[1].size
+    for i in range(number):
+        vectors = total[0, i * 6 * local : (i + 1) * 6 * local].reshape(6, local)
+        at = first + i * bias_size
+        bias = total[0, at : at + bias_size].reshape(shapes[0].shape)
+        at = first + number * bias_size + i * hidden_size
+        hidden_bias = total[0, at : at + hidden_size].reshape(shapes[1].shape)
+        result.append((vectors, bias, hidden_bias))
+    return result
+
+
+def order_matrix(width, y_index, z_index):
+    count = lax.axis_size("dp")
+    rows = width // (2 * count)
+    natural = lax.broadcasted_iota(jnp.int32, (width, width), 0)
+    place = lax.broadcasted_iota(jnp.int32, (width, width), 1)
+    half, rest = place // (width // 2), place % (width // 2)
+    step, inner = rest // rows, rest % rows
+    wanted = ((z_index - step) % count) * (2 * rows) + (half ^ y_index) * rows + inner
+    return (natural == wanted).astype(BF16)
+
+
+def my_rows(pair, y_index):
+    own = jnp.where(y_index == 0, pair[0], pair[1])
+    sent = jnp.where(y_index == 0, pair[1], pair[0])
+    return own, cross_y(sent)
+
+
+def fast_shards(inputs, segments, cotangent, *params):
+    y_index = lax.axis_index("ctx")
+    z_index = lax.axis_index("dp")
+    me = lax.axis_index("tp")
+    tokens, features = inputs.shape[1], inputs.shape[2]
+    length = segments.shape[1] * 2
+    doc_max = min(DOC_MAX, length // 2)
+    blocks = (params[:12], params[12:])
+    vectors = fetch_vectors(
+        [((p[0], p[1], p[5], p[6], p[7], p[11]), p[3], p[9]) for p in blocks], y_index, z_index
+    )
+    weights = [fetch_matrices((p[2], p[4], p[8], p[10]), y_index) for p in blocks]
+    chooser = order_matrix(features, y_index, z_index)
+    own, other = my_rows(inputs, y_index)
+    stream = times(y_order(own, other, y_index, 0), chooser)
+    own, other = my_rows(cotangent, y_index)
+    grad_out = times(y_order(own, other, y_index, 0), chooser)
+    own, other = my_rows(segments, y_index)
+    docs = y_order(own, other, y_index, 0)
+    row_docs, column_docs = docs.reshape(length, 1), docs.reshape(1, length)
+    me_list = me.astype(jnp.int32).reshape(1)
+    context = (me_list, row_docs, column_docs, doc_max)
+    middle_stream, student_saved = fast_forward(stream, weights[0], vectors[0], *context)
+    final_stream, teacher_saved = fast_forward(middle_stream, weights[1], vectors[1], *context)
+    grad_between, teacher_small, teacher_large = fast_backward(
+        grad_out, teacher_saved, weights[1], vectors[1], *context, y_index
+    )
+    grad_in, student_small, student_large = fast_backward(
+        grad_between, student_saved, weights[0], vectors[0], *context, y_index
+    )
+    small = return_vectors(
+        [student_small, teacher_small], (params[3], params[9]), y_index, z_index
+    )
+
+    def restore(value):
+        first, second = value[:tokens], value[tokens:]
+        kept = jnp.where(y_index == 0, first, second)
+        sent = jnp.where(y_index == 0, second, first)
+        received = cross_y(sent)
+        return jnp.where(
+            y_index == 0, jnp.stack([kept, received]), jnp.stack([received, kept])
+        )
+
+    final = times_across(final_stream.astype(BF16), chooser, BF16)
+    input_grad = lax.dot_general(
+        grad_in,
+        chooser.astype(F32),
+        (((1,), (1,)), ((), ())),
+        precision=lax.Precision.HIGHEST,
+        preferred_element_type=F32,
+    )
+    outputs = [restore(final), restore(input_grad)]
+    for (sums, bias, hidden_bias), (pack, expand, reduce), p in zip(
+        small, (student_large, teacher_large), blocks
+    ):
+        wide = p[2].shape[1] * p[2].shape[2]
+        outputs += [
+            sums[0],
+            sums[1],
+            pack[:, :wide].reshape(p[2].shape),
+            bias,
+            pack[:, wide:].T,
+            sums[2],
+            sums[3],
+            sums[4],
+            expand,
+            hidden_bias,
+            reduce.T,
+            sums[5],
+        ]
+    return tuple(outputs)
+
+
 def solution(mesh):
+    quick = mesh.shape["ctx"] == 2 and mesh.shape["tp"] == 4
     placed = (
         P("dp", ("ctx", "tp"), None),
         P("dp", "ctx"),
@@ -558,7 +1147,7 @@
         P("dp"),
     )
     return jax.shard_map(
-        shards,
+        fast_shards if quick else general_shards,
         mesh=mesh,
         in_specs=placed,
         out_specs=(

time: 1210 us -> 694 us (0.57)
  waiting for transfers between devices: 566 us -> 275 us
  blocking collectives: 197 us -> 0 us
  matrix products: 246 us -> 89.8 us
  starting transfers between devices: 18.3 us -> 123 us
  Pallas kernels: 0 us -> 31 us
  local copies, waits for them, and re-layouts: 75.1 us -> 100 us
  between operations: 19 us -> 3.83 us
  other arithmetic: 73.2 us -> 60.3 us
    reduce_scatter x14 -> x0, waiting for transfers between devices: 268 us -> none  [the longest x8 198 us: gather_sums(): lax.psum_scatter(partial_value.astype(jnp.bfloat16), 'tp', scatter_dimens...]
    ppermute x9 -> x98, waiting for transfers between devices: 45.7 us -> 275 us  [the longest x42 152 us: shift_z(): lax.ppermute(value, 'dp', [(i, (i + distance) % count) for i in range(cou...]
    all_gather x12 -> x0, waiting for transfers between devices: 172 us -> none  [the longest x8 103 us: spread_rows(): return lax.all_gather(row_block, 'tp', axis=1, tiled=True)]
    dot_general x108 -> x35, matrix products: 246 us -> 89.8 us  [the longest x16 37.6 us: times_across(): lax.dot_general(left, right, (((1,), (1,)), ((), ())), preferred_element_...]
    all_gather x8 -> x0, blocking collectives: 138 us -> none  [the longest x2 54.2 us: layer_forward(): lax.all_gather(merged_weight, 'dp', axis=0, tiled=True)]
    ppermute x9 -> x98, starting transfers between devices: 16.7 us -> 123 us  [the longest x42 82.9 us: shift_z(): lax.ppermute(value, 'dp', [(i, (i + distance) % count) for i in range(cou...]
    unnamed x39 -> x0, waiting for transfers between devices: 79.8 us -> none
    unnamed x2 -> x0, blocking collectives: 40.5 us -> none
  transfers between devices with their start and end apart: 42 -> 98, of which waited for: 31 -> 36; matrix products, arithmetic and copies ran while one was open for 15% -> 30% of each run, Pallas kernels for 0% -> 5%
where the time goes in v1:
time: 694 us; the launch traced here: 683 us
  waiting for transfers between devices  275 us (40%)
  starting transfers between devices  123 us (18%)
  local copies, waits for them, and re-layouts  100 us (14%)
  matrix products  89.8 us (13%)
  other arithmetic  60.3 us (9%)
  Pallas kernels  31 us (4%)
    ppermute x42, waiting for transfers between devices, shift_z(): lax.ppermute(value, 'dp', [(i, (i + distance) % count) for i in range(cou...  152 us
    ppermute x56, waiting for transfers between devices, swap(): return lax.ppermute(value, axis, route)  123 us
    ppermute x42, starting transfers between devices, shift_z(): lax.ppermute(value, 'dp', [(i, (i + distance) % count) for i in range(cou...  82.9 us
    ppermute x56, starting transfers between devices, swap(): return lax.ppermute(value, axis, route)  40.1 us
    dot_general x16, matrix products, times_across(): lax.dot_general(left, right, (((1,), (1,)), ((), ())), preferred_element_...  37.6 us
    unnamed x340, local copies, waits for them, and re-layouts  36.4 us
    dot_general x10, matrix products, times(): return jnp.dot(left, right, preferred_element_type=F32).astype(kind)  34.5 us
    pallas_call x2, Pallas kernels, attention_backward(): pl.pallas_call(body, out_shape=jax.ShapeDtypeStruct((length, 3 * width),...  19.4 us
  transfers between devices with their start and end apart: 98, of which 36 were waited for; matrix products, arithmetic and copies ran while one was open for 30% of the time, Pallas kernels for 5%

profile of v1, /device:TPU:0, one launch (start us, length us, event | category | flops | bytes accessed | tf_op | source)
XLA Modules:
  0.0 683.2 jit_solution(6948508614231032996)
XLA Ops:
  11.9 5.1 collective-permute-start.3
  22.5 2.9 collective-permute-start.8
  33.8 3.7 collective-permute-start.22
  46.6 3.3 collective-permute-done.4
  52.9 8.3 %collective-permute-done.9 = bf16[384,768]{0,1:T(8,128)(2,1)} collective-permute-done((bf16[384,768]{0,1:T(8,128)(2,1)S(1)}, bf16[384,768]{0,1:T(8,128)(2,1)}, u32[]{:S(2)}, u32[]{:S(2)}) %collective-permute-start.9) | collective-permute-done | bytes 589856 | tf_op jit(solution)/shard_map/ppermute | solution.py:541
  63.5 3.1 add_convert_fusion.1.refs_1_
  66.7 5.8 attention_forward.2
  76.1 6.1 collective-permute-start.15
  86.2 4.0 collective-permute-start.21
  90.2 19.1 %collective-permute-done.15 = bf16[96,768]{0,1:T(8,128)(2,1)} collective-permute-done((bf16[96,768]{0,1:T(8,128)(2,1)}, bf16[96,768]{0,1:T(8,128)(2,1)}, u32[]{:S(2)}, u32[]{:S(2)}) %collective-permute-start.15) | collective-permute-done | bytes 147488 | tf_op jit(solution)/shard_map/ppermute | solution.py:558
  115.1 10.8 %collective-permute-done.21 = bf16[192,768]{0,1:T(8,128)(2,1)S(1)} collective-permute-done((bf16[192,768]{0,1:T(8,128)(2,1)}, bf16[192,768]{0,1:T(8,128)(2,1)S(1)}, u32[]{:S(2)}, u32[]{:S(2)}) %collective-permute-start.21) | collective-permute-done | bytes 294944 | tf_op jit(solution)/shard_map/ppermute | solution.py:558
  131.2 3.2 concatenate.282
  135.0 2.8 pad_maximum_fusion.8
  138.3 3.4 collective-permute-done.12
  146.4 19.5 %collective-permute-done.19 = bf16[2,768]{1,0:T(2,128)(2,1)S(1)} collective-permute-done((bf16[2,768]{1,0:T(2,128)(2,1)S(1)}, bf16[2,768]{1,0:T(2,128)(2,1)S(1)}, u32[]{:S(2)}, u32[]{:S(2)}) %collective-permute-start.19) | collective-permute-done | bytes 3104 | tf_op jit(solution)/shard_map/ppermute | solution.py:541
  166.6 5.6 multiply_convert_fusion.1
  172.2 3.0 convolution_convert_fusion.16
  177.0 2.8 fusion.213
  185.2 6.3 collective-permute-done.25
  192.5 7.9 %collective-permute-done.28 = bf16[96,768]{0,1:T(8,128)(2,1)S(1)} collective-permute-done((bf16[96,768]{0,1:T(8,128)(2,1)S(1)}, bf16[96,768]{0,1:T(8,128)(2,1)S(1)}, u32[]{:S(2)}, u32[]{:S(2)}) %collective-permute-start.28) | collective-permute-done | bytes 147488 | tf_op jit(solution)/shard_map/ppermute | solution.py:558
  206.8 3.2 collective-permute-start.35
  213.0 3.4 collective-permute-done.30
  220.5 3.2 add_convert_fusion.refs_1_
  223.7 5.8 attention_forward.3
  237.8 3.3 collective-permute-start.40
  248.5 19.5 %collective-permute-done.40 = bf16[192,768]{0,1:T(8,128)(2,1)S(1)} collective-permute-done((bf16[192,768]{0,1:T(8,128)(2,1)}, bf16[192,768]{0,1:T(8,128)(2,1)S(1)}, u32[]{:S(2)}, u32[]{:S(2)}) %collective-permute-start.40) | collective-permute-done | bytes 294944 | tf_op jit(solution)/shard_map/ppermute | solution.py:558
  272.3 3.9 concatenate.296
  280.2 3.4 collective-permute-done.32
  284.5 2.7 fusion.214
  287.7 19.2 %collective-permute-done.38 = bf16[384,1536]{0,1:T(8,128)(2,1)S(1)} collective-permute-done((bf16[384,1536]{0,1:T(8,128)(2,1)S(1)}, bf16[384,1536]{0,1:T(8,128)(2,1)S(1)}, u32[]{:S(2)}, u32[]{:S(2)}) %collective-permute-start.38) | collective-permute-done | bytes 1179680 | tf_op jit(solution)/shard_map/ppermute | solution.py:541
  306.9 4.1 multiply_convert_fusion
  311.1 2.9 convolution_convert_fusion.15
  314.1 4.8 convert_reduce_fusion
  319.0 3.6 convolution_convert_fusion.13
  327.9 3.2 convolution_convert_fusion.14
  331.8 3.4 multiply_reduce_fusion
  344.3 19.4 %collective-permute-done.48 = bf16[256,768]{1,0:T(8,128)(2,1)S(1)} collective-permute-done((bf16[256,768]{1,0:T(8,128)(2,1)S(1)}, bf16[256,768]{1,0:T(8,128)(2,1)S(1)}, u32[]{:S(2)}, u32[]{:S(2)}) %collective-permute-start.48) | collective-permute-done | bytes 393248 | tf_op jit(solution)/shard_map/ppermute | solution.py:541
  366.6 3.9 collective-permute-start.94
  372.4 18.8 %collective-permute-done.95 = bf16[192,768]{0,1:T(8,128)(2,1)S(1)} collective-permute-done((bf16[192,768]{0,1:T(8,128)(2,1)S(1)}, bf16[192,768]{0,1:T(8,128)(2,1)S(1)}, u32[]{:S(2)}, u32[]{:S(2)}) %collective-permute-start.95) | collective-permute-done | bytes 294944 | tf_op jit(solution)/shard_map/ppermute | solution.py:558
  391.2 4.8 collective-permute-done.94
  403.1 9.7 %attention_backward.2 = bf16[1024,576]{1,0:T(8,128)(2,1)S(1)} custom-call(s32[1]{0:T(128)} %bitcast.3.refs_0_, bf16[1024,576]{1,0:T(8,128)(2,1)S(1)} %copy-done.3, s32[1024,1]{1,0:T(8,128)S(1)} %broadcast_select_fusion.refs_2_, s32[1,1024]{1,0:T(1,128)S(1)} %broadcast_select_fusion.11.refs_3_, f32[1024,3]{1,0:T(8,128)S(1)} %copy-done.7, ...), custom_call_target="tpu_custom_call" | custom-call | flops 4026531840 | bytes 3145728 | tf_op jit(solution)/shard_map/attention_backward/pallas_call | solution.py:737
  414.2 2.8 convolution_convert_fusion.4
  429.5 3.5 collective-permute-start.91
  435.8 3.0 collective-permute-start.83
  441.1 6.9 %collective-permute-start.84 = (bf16[96,768]{0,1:T(8,128)(2,1)S(1)}, bf16[96,768]{0,1:T(8,128)(2,1)S(1)}, u32[]{:S(2)}, u32[]{:S(2)}) collective-permute-start(bf16[96,768]{0,1:T(8,128)(2,1)S(1)} %get-tuple-element.234), channel_id=1, source_target_pairs={{0,16},{8,24},{16,0},{24,8},{1,17},{9,25},{17,1},{25,9},{2,18},{10... | collective-permute-start | bytes 442376 | tf_op jit(solution)/shard_map/ppermute | solution.py:558
  449.4 11.7 %collective-permute-done.90 = bf16[96,768]{0,1:T(8,128)(2,1)S(1)} collective-permute-done((bf16[96,768]{0,1:T(8,128)(2,1)S(1)}, bf16[96,768]{0,1:T(8,128)(2,1)S(1)}, u32[]{:S(2)}, u32[]{:S(2)}) %collective-permute-start.90) | collective-permute-done | bytes 147488 | tf_op jit(solution)/shard_map/ppermute | solution.py:558
  461.8 7.3 %collective-permute-done.84 = bf16[96,768]{0,1:T(8,128)(2,1)S(1)} collective-permute-done((bf16[96,768]{0,1:T(8,128)(2,1)S(1)}, bf16[96,768]{0,1:T(8,128)(2,1)S(1)}, u32[]{:S(2)}, u32[]{:S(2)}) %collective-permute-start.84) | collective-permute-done | bytes 147488 | tf_op jit(solution)/shard_map/ppermute | solution.py:558
  472.9 3.0 collective-permute-done.86
  479.7 6.4 convert_reduce_fusion.1
  499.5 3.4 multiply_reduce_fusion.2
  510.1 25.2 %collective-permute-done.54 = bf16[256,768]{1,0:T(8,128)(2,1)} collective-permute-done((bf16[256,768]{1,0:T(8,128)(2,1)}, bf16[256,768]{1,0:T(8,128)(2,1)}, u32[]{:S(2)}, u32[]{:S(2)}) %collective-permute-start.54) | collective-permute-done | bytes 393248 | tf_op jit(solution)/shard_map/ppermute | solution.py:541
  539.4 3.9 collective-permute-start.78
  546.4 17.6 %collective-permute-done.79 = bf16[192,768]{0,1:T(8,128)(2,1)S(1)} collective-permute-done((bf16[192,768]{0,1:T(8,128)(2,1)S(1)}, bf16[192,768]{0,1:T(8,128)(2,1)S(1)}, u32[]{:S(2)}, u32[]{:S(2)}) %collective-permute-start.79) | collective-permute-done | bytes 294944 | tf_op jit(solution)/shard_map/ppermute | solution.py:558
  564.1 4.8 collective-permute-done.78
  575.8 9.7 %attention_backward.3 = bf16[1024,576]{1,0:T(8,128)(2,1)S(1)} custom-call(s32[1]{0:T(128)} %bitcast.3.refs_0_, bf16[1024,576]{1,0:T(8,128)(2,1)S(1)} %copy-done.1, s32[1024,1]{1,0:T(8,128)S(1)} %broadcast_select_fusion.refs_2_, s32[1,1024]{1,0:T(1,128)S(1)} %broadcast_select_fusion.11.refs_3_, f32[1024,3]{1,0:T(8,128)S(1)} %copy-done.5, ...), custom_call_target="tpu_custom_call" | custom-call | flops 4026531840 | bytes 3145728 | tf_op jit(solution)/shard_map/attention_backward/pallas_call | solution.py:737
  588.7 2.7 convolution_convert_fusion.5
  604.8 3.6 collective-permute-start.75
  608.3 2.9 collective-permute-start.74
  616.0 4.7 collective-permute-done.75
  620.7 5.2 collective-permute-start.68
  628.8 4.6 collective-permute-done.69
  633.4 11.2 %collective-permute-done.68 = bf16[96,768]{0,1:T(8,128)(2,1)S(1)} collective-permute-done((bf16[96,768]{0,1:T(8,128)(2,1)S(1)}, bf16[96,768]{0,1:T(8,128)(2,1)S(1)}, u32[]{:S(2)}, u32[]{:S(2)}) %collective-permute-start.68) | collective-permute-done | bytes 147488 | tf_op jit(solution)/shard_map/ppermute | solution.py:558
  663.1 2.9 collective-permute-done.60
  667.9 2.7 fusion.43
  (774 shorter events, 256.6 us)
Async XLA Ops:
  11.9 21.3 %collective-permute-start.3 = (bf16[1,2880]{1,0:T(2,128)(2,1)S(1)}, bf16[1,2880]{1,0:T(2,128)(2,1)S(1)}, u32[]{:S(2)}, u32[]{:S(2)}) collective-permute-start(bf16[1,2880]{1,0:T(2,128)(2,1)S(1)} %concatenate.260), channel_id=1, source_target_pairs={{0,24},{8,0},{16,8},{24,16},{1,25},{9,1},{17,9},{25,17},{2,26},{10... | collective-permute-start | bytes 17288 | tf_op jit(solution)/shard_map/ppermute | solution.py:558
  17.0 16.2 %collective-permute-start.2 = (bf16[1,2880]{1,0:T(2,128)(2,1)S(1)}, bf16[1,2880]{1,0:T(2,128)(2,1)S(1)}, u32[]{:S(2)}, u32[]{:S(2)}) collective-permute-start(bf16[1,2880]{1,0:T(2,128)(2,1)S(1)} %concatenate.260), channel_id=1, source_target_pairs={{0,16},{8,24},{16,0},{24,8},{1,17},{9,25},{17,1},{25,9},{2,18},{10... | collective-permute-start | bytes 17288 | tf_op jit(solution)/shard_map/ppermute | solution.py:558
  17.0 16.8 %collective-permute-start.1 = (bf16[1,2880]{1,0:T(2,128)(2,1)S(1)}, bf16[1,2880]{1,0:T(2,128)(2,1)S(1)}, u32[]{:S(2)}, u32[]{:S(2)}) collective-permute-start(bf16[1,2880]{1,0:T(2,128)(2,1)S(1)} %concatenate.260), channel_id=1, source_target_pairs={{0,8},{8,16},{16,24},{24,0},{1,9},{9,17},{17,25},{25,1},{2,10},{10... | collective-permute-start | bytes 17288 | tf_op jit(solution)/shard_map/ppermute | solution.py:558
  22.5 20.6 %collective-permute-start.8 = (bf16[96,768]{0,1:T(8,128)(2,1)S(1)}, bf16[96,768]{0,1:T(8,128)(2,1)S(1)}, u32[]{:S(2)}, u32[]{:S(2)}) collective-permute-start(bf16[96,768]{0,1:T(8,128)(2,1)S(1)} %fusion.119), channel_id=1, source_target_pairs={{0,24},{8,0},{16,8},{24,16},{1,25},{9,1},{17,9},{25,17},{2,26},{10... | collective-permute-start | bytes 442376 | tf_op jit(solution)/shard_map/ppermute | solution.py:558
  33.8 79.4 %collective-permute-start.22 = (bf16[192,768]{0,1:T(8,128)(2,1)}, bf16[192,768]{0,1:T(8,128)(2,1)}, u32[]{:S(2)}, u32[]{:S(2)}) collective-permute-start(bf16[192,768]{0,1:T(8,128)(2,1)} %pad_maximum_fusion.56), channel_id=1, source_target_pairs={{0,24},{8,0},{16,8},{24,16},{1,25},{9,1},{17,9},{25,17},{2,26},{10... | collective-permute-start | bytes 884744 | tf_op jit(solution)/shard_map/ppermute | solution.py:558
  73.7 53.0 %collective-permute-start.11 = (bf16[512,768]{1,0:T(8,128)(2,1)}, bf16[512,768]{1,0:T(8,128)(2,1)}, u32[]{:S(2)}, u32[]{:S(2)}) collective-permute-start(bf16[512,768]{1,0:T(8,128)(2,1)} %convolution_convert_fusion.9), channel_id=1, source_target_pairs={{0,1},{1,0},{2,3},{3,2},{4,5},{5,4},{6,7},{7,6},{8,9},{9,8},{10,11... | collective-permute-start | bytes 2359304 | tf_op jit(solution)/shard_map/ppermute | solution.py:541
  76.1 33.2 %collective-permute-start.15 = (bf16[96,768]{0,1:T(8,128)(2,1)}, bf16[96,768]{0,1:T(8,128)(2,1)}, u32[]{:S(2)}, u32[]{:S(2)}) collective-permute-start(bf16[96,768]{0,1:T(8,128)(2,1)} %broadcast_select_fusion.6), channel_id=1, source_target_pairs={{0,16},{8,24},{16,0},{24,8},{1,17},{9,25},{17,1},{25,9},{2,18},{10... | collective-permute-start | bytes 442376 | tf_op jit(solution)/shard_map/ppermute | solution.py:558
  82.2 27.1 %collective-permute-start.14 = (bf16[96,768]{0,1:T(8,128)(2,1)}, bf16[96,768]{0,1:T(8,128)(2,1)}, u32[]{:S(2)}, u32[]{:S(2)}) collective-permute-start(bf16[96,768]{0,1:T(8,128)(2,1)} %broadcast_select_fusion.6), channel_id=1, source_target_pairs={{0,8},{8,16},{16,24},{24,0},{1,9},{9,17},{17,25},{25,1},{2,10},{10... | collective-permute-start | bytes 442376 | tf_op jit(solution)/shard_map/ppermute | solution.py:558
  86.2 39.7 %collective-permute-start.21 = (bf16[192,768]{0,1:T(8,128)(2,1)}, bf16[192,768]{0,1:T(8,128)(2,1)S(1)}, u32[]{:S(2)}, u32[]{:S(2)}) collective-permute-start(bf16[192,768]{0,1:T(8,128)(2,1)} %pad_maximum_fusion.56), channel_id=1, source_target_pairs={{0,16},{8,24},{16,0},{24,8},{1,17},{9,25},{17,1},{25,9},{2,18},{10... | collective-permute-start | bytes 884744 | tf_op jit(solution)/shard_map/ppermute | solution.py:558
  109.3 21.7 %collective-permute-start.20 = (bf16[192,768]{0,1:T(8,128)(2,1)}, bf16[192,768]{0,1:T(8,128)(2,1)S(1)}, u32[]{:S(2)}, u32[]{:S(2)}) collective-permute-start(bf16[192,768]{0,1:T(8,128)(2,1)} %pad_maximum_fusion.56), channel_id=1, source_target_pairs={{0,8},{8,16},{16,24},{24,0},{1,9},{9,17},{17,25},{25,1},{2,10},{10... | collective-permute-start | bytes 884744 | tf_op jit(solution)/shard_map/ppermute | solution.py:558
  111.7 23.2 %collective-permute-start.17 = (bf16[384,768]{0,1:T(8,128)(2,1)}, bf16[384,768]{0,1:T(8,128)(2,1)}, u32[]{:S(2)}, u32[]{:S(2)}) collective-permute-start(bf16[384,768]{0,1:T(8,128)(2,1)} %pad_maximum_fusion.45), channel_id=1, source_target_pairs={{0,2},{1,3},{2,0},{3,1},{4,6},{5,7},{6,4},{7,5},{8,10},{9,11},{10,... | collective-permute-start | bytes 1769480 | tf_op jit(solution)/shard_map/ppermute | solution.py:541
  134.4 37.8 %collective-permute-start.23 = (bf16[768,768]{0,1:T(8,128)(2,1)}, bf16[768,768]{0,1:T(8,128)(2,1)}, u32[]{:S(2)}, u32[]{:S(2)}) collective-permute-start(bf16[768,768]{0,1:T(8,128)(2,1)} %concatenate.282), channel_id=1, source_target_pairs={{0,2},{1,3},{2,0},{3,1},{4,6},{5,7},{6,4},{7,5},{8,10},{9,11},{10,... | collective-permute-start | bytes 3538952 | tf_op jit(solution)/shard_map/ppermute | solution.py:541
  137.8 28.8 %collective-permute-start.18 = (bf16[384,1536]{0,1:T(8,128)(2,1)}, bf16[384,1536]{0,1:T(8,128)(2,1)}, u32[]{:S(2)}, u32[]{:S(2)}) collective-permute-start(bf16[384,1536]{0,1:T(8,128)(2,1)} %pad_maximum_fusion.8), channel_id=1, source_target_pairs={{0,4},{4,0},{1,5},{5,1},{2,6},{6,2},{3,7},{7,3},{8,12},{12,8},{9,1... | collective-permute-start | bytes 3538952 | tf_op jit(solution)/shard_map/ppermute | solution.py:541
  143.4 23.1 %collective-permute-start.13 = (bf16[256,768]{1,0:T(8,128)(2,1)S(1)}, bf16[256,768]{1,0:T(8,128)(2,1)S(1)}, u32[]{:S(2)}, u32[]{:S(2)}) collective-permute-start(bf16[256,768]{1,0:T(8,128)(2,1)S(1)} %add_convert_fusion.5), channel_id=1, source_target_pairs={{0,1},{1,0},{2,3},{3,2},{4,5},{5,4},{6,7},{7,6},{8,9},{9,8},{10,11... | collective-permute-start | bytes 1179656 | tf_op jit(solution)/shard_map/ppermute | solution.py:541
  144.7 21.2 %collective-permute-start.19 = (bf16[2,768]{1,0:T(2,128)(2,1)S(1)}, bf16[2,768]{1,0:T(2,128)(2,1)S(1)}, u32[]{:S(2)}, u32[]{:S(2)}) collective-permute-start(bf16[2,768]{1,0:T(2,128)(2,1)S(1)} %pad_maximum_fusion.71), channel_id=1, source_target_pairs={{0,2},{1,3},{2,0},{3,1},{4,6},{5,7},{6,4},{7,5},{8,10},{9,11},{10,... | collective-permute-start | bytes 9224 | tf_op jit(solution)/shard_map/ppermute | solution.py:541
  183.2 17.2 %collective-permute-start.28 = (bf16[96,768]{0,1:T(8,128)(2,1)S(1)}, bf16[96,768]{0,1:T(8,128)(2,1)S(1)}, u32[]{:S(2)}, u32[]{:S(2)}) collective-permute-start(bf16[96,768]{0,1:T(8,128)(2,1)S(1)} %fusion.117), channel_id=1, source_target_pairs={{0,16},{8,24},{16,0},{24,8},{1,17},{9,25},{17,1},{25,9},{2,18},{10... | collective-permute-start | bytes 442376 | tf_op jit(solution)/shard_map/ppermute | solution.py:558
  183.3 17.1 %collective-permute-start.27 = (bf16[96,768]{0,1:T(8,128)(2,1)S(1)}, bf16[96,768]{0,1:T(8,128)(2,1)S(1)}, u32[]{:S(2)}, u32[]{:S(2)}) collective-permute-start(bf16[96,768]{0,1:T(8,128)(2,1)S(1)} %fusion.117), channel_id=1, source_target_pairs={{0,8},{8,16},{16,24},{24,0},{1,9},{9,17},{17,25},{25,1},{2,10},{10... | collective-permute-start | bytes 442376 | tf_op jit(solution)/shard_map/ppermute | solution.py:558
  192.5 28.0 %collective-permute-start.26 = (bf16[512,768]{1,0:T(8,128)(2,1)}, bf16[512,768]{1,0:T(8,128)(2,1)}, u32[]{:S(2)}, u32[]{:S(2)}) collective-permute-start(bf16[512,768]{1,0:T(8,128)(2,1)} %pad_maximum_fusion.12), channel_id=1, source_target_pairs={{0,1},{1,0},{2,3},{3,2},{4,5},{5,4},{6,7},{7,6},{8,9},{9,8},{10,11... | collective-permute-start | bytes 2359304 | tf_op jit(solution)/shard_map/ppermute | solution.py:541
  206.7 31.1 %collective-permute-start.36 = (bf16[96,768]{0,1:T(8,128)(2,1)}, bf16[96,768]{0,1:T(8,128)(2,1)}, u32[]{:S(2)}, u32[]{:S(2)}) collective-permute-start(bf16[96,768]{0,1:T(8,128)(2,1)} %broadcast_select_fusion.3), channel_id=1, source_target_pairs={{0,24},{8,0},{16,8},{24,16},{1,25},{9,1},{17,9},{25,17},{2,26},{10... | collective-permute-start | bytes 442376 | tf_op jit(solution)/shard_map/ppermute | solution.py:558
  206.8 34.4 %collective-permute-start.35 = (bf16[96,768]{0,1:T(8,128)(2,1)}, bf16[96,768]{0,1:T(8,128)(2,1)}, u32[]{:S(2)}, u32[]{:S(2)}) collective-permute-start(bf16[96,768]{0,1:T(8,128)(2,1)} %broadcast_select_fusion.3), channel_id=1, source_target_pairs={{0,16},{8,24},{16,0},{24,8},{1,17},{9,25},{17,1},{25,9},{2,18},{10... | collective-permute-start | bytes 442376 | tf_op jit(solution)/shard_map/ppermute | solution.py:558
  210.0 33.2 %collective-permute-start.34 = (bf16[96,768]{0,1:T(8,128)(2,1)}, bf16[96,768]{0,1:T(8,128)(2,1)}, u32[]{:S(2)}, u32[]{:S(2)}) collective-permute-start(bf16[96,768]{0,1:T(8,128)(2,1)} %broadcast_select_fusion.3), channel_id=1, source_target_pairs={{0,8},{8,16},{16,24},{24,0},{1,9},{9,17},{17,25},{25,1},{2,10},{10... | collective-permute-start | bytes 442376 | tf_op jit(solution)/shard_map/ppermute | solution.py:558
  217.2 28.9 %collective-permute-start.41 = (bf16[192,768]{0,1:T(8,128)(2,1)}, bf16[192,768]{0,1:T(8,128)(2,1)}, u32[]{:S(2)}, u32[]{:S(2)}) collective-permute-start(bf16[192,768]{0,1:T(8,128)(2,1)} %pad_maximum_fusion.57), channel_id=1, source_target_pairs={{0,24},{8,0},{16,8},{24,16},{1,25},{9,1},{17,9},{25,17},{2,26},{10... | collective-permute-start | bytes 884744 | tf_op jit(solution)/shard_map/ppermute | solution.py:558
  231.6 37.3 %collective-permute-start.31 = (bf16[512,768]{1,0:T(8,128)(2,1)}, bf16[512,768]{1,0:T(8,128)(2,1)}, u32[]{:S(2)}, u32[]{:S(2)}) collective-permute-start(bf16[512,768]{1,0:T(8,128)(2,1)} %convolution_convert_fusion.8), channel_id=1, source_target_pairs={{0,1},{1,0},{2,3},{3,2},{4,5},{5,4},{6,7},{7,6},{8,9},{9,8},{10,11... | collective-permute-start | bytes 2359304 | tf_op jit(solution)/shard_map/ppermute | solution.py:541
  237.8 30.2 %collective-permute-start.40 = (bf16[192,768]{0,1:T(8,128)(2,1)}, bf16[192,768]{0,1:T(8,128)(2,1)S(1)}, u32[]{:S(2)}, u32[]{:S(2)}) collective-permute-start(bf16[192,768]{0,1:T(8,128)(2,1)} %pad_maximum_fusion.57), channel_id=1, source_target_pairs={{0,16},{8,24},{16,0},{24,8},{1,17},{9,25},{17,1},{25,9},{2,18},{10... | collective-permute-start | bytes 884744 | tf_op jit(solution)/shard_map/ppermute | solution.py:558
  241.2 30.9 %collective-permute-start.39 = (bf16[192,768]{0,1:T(8,128)(2,1)}, bf16[192,768]{0,1:T(8,128)(2,1)S(1)}, u32[]{:S(2)}, u32[]{:S(2)}) collective-permute-start(bf16[192,768]{0,1:T(8,128)(2,1)} %pad_maximum_fusion.57), channel_id=1, source_target_pairs={{0,8},{8,16},{16,24},{24,0},{1,9},{9,17},{17,25},{25,1},{2,10},{10... | collective-permute-start | bytes 884744 | tf_op jit(solution)/shard_map/ppermute | solution.py:558
  243.2 41.2 %collective-permute-start.45 = (bf16[128,768]{1,0:T(8,128)(2,1)}, bf16[128,768]{1,0:T(8,128)(2,1)}, u32[]{:S(2)}, u32[]{:S(2)}) collective-permute-start(bf16[128,768]{1,0:T(8,128)(2,1)} %get-tuple-element.246), channel_id=1, source_target_pairs={{0,4},{4,0},{1,5},{5,1},{2,6},{6,2},{3,7},{7,3},{8,12},{12,8},{9,1... | collective-permute-start | bytes 589832 | tf_op jit(solution)/shard_map/ppermute | solution.py:541
  246.1 31.7 %collective-permute-start.37 = (bf16[384,768]{0,1:T(8,128)(2,1)}, bf16[384,768]{0,1:T(8,128)(2,1)}, u32[]{:S(2)}, u32[]{:S(2)}) collective-permute-start(bf16[384,768]{0,1:T(8,128)(2,1)} %pad_maximum_fusion.47), channel_id=1, source_target_pairs={{0,2},{1,3},{2,0},{3,1},{4,6},{5,7},{6,4},{7,5},{8,10},{9,11},{10,... | collective-permute-start | bytes 1769480 | tf_op jit(solution)/shard_map/ppermute | solution.py:541
  276.2 34.8 %collective-permute-start.42 = (bf16[768,768]{0,1:T(8,128)(2,1)}, bf16[768,768]{0,1:T(8,128)(2,1)S(1)}, u32[]{:S(2)}, u32[]{:S(2)}) collective-permute-start(bf16[768,768]{0,1:T(8,128)(2,1)} %concatenate.296), channel_id=1, source_target_pairs={{0,2},{1,3},{2,0},{3,1},{4,6},{5,7},{6,4},{7,5},{8,10},{9,11},{10,... | collective-permute-start | bytes 3538952 | tf_op jit(solution)/shard_map/ppermute | solution.py:541
  279.6 27.3 %collective-permute-start.38 = (bf16[384,1536]{0,1:T(8,128)(2,1)S(1)}, bf16[384,1536]{0,1:T(8,128)(2,1)S(1)}, u32[]{:S(2)}, u32[]{:S(2)}) collective-permute-start(bf16[384,1536]{0,1:T(8,128)(2,1)S(1)} %pad_maximum_fusion.9), channel_id=1, source_target_pairs={{0,4},{4,0},{1,5},{5,1},{2,6},{6,2},{3,7},{7,3},{8,12},{12,8},{9,1... | collective-permute-start | bytes 3538952 | tf_op jit(solution)/shard_map/ppermute | solution.py:541
  284.3 22.6 %collective-permute-start.33 = (bf16[256,768]{1,0:T(8,128)(2,1)S(1)}, bf16[256,768]{1,0:T(8,128)(2,1)S(1)}, u32[]{:S(2)}, u32[]{:S(2)}) collective-permute-start(bf16[256,768]{1,0:T(8,128)(2,1)S(1)} %add_convert_fusion.3), channel_id=1, source_target_pairs={{0,1},{1,0},{2,3},{3,2},{4,5},{5,4},{6,7},{7,6},{8,9},{9,8},{10,11... | collective-permute-start | bytes 1179656 | tf_op jit(solution)/shard_map/ppermute | solution.py:541
  287.2 26.9 %collective-permute-start.46 = (bf16[256,768]{1,0:T(8,128)(2,1)S(1)}, bf16[256,768]{1,0:T(8,128)(2,1)S(1)}, u32[]{:S(2)}, u32[]{:S(2)}) collective-permute-start(bf16[256,768]{1,0:T(8,128)(2,1)S(1)} %get-tuple-element.328), channel_id=1, source_target_pairs={{0,1},{1,0},{2,3},{3,2},{4,5},{5,4},{6,7},{7,6},{8,9},{9,8},{10,11... | collective-permute-start | bytes 1179656 | tf_op jit(solution)/shard_map/ppermute | solution.py:541
  327.2 36.7 %collective-permute-start.93 = (bf16[768,768]{0,1:T(8,128)(2,1)}, bf16[768,768]{0,1:T(8,128)(2,1)}, u32[]{:S(2)}, u32[]{:S(2)}) collective-permute-start(bf16[768,768]{0,1:T(8,128)(2,1)} %slice.920), channel_id=1, source_target_pairs={{0,2},{1,3},{2,0},{3,1},{4,6},{5,7},{6,4},{7,5},{8,10},{9,11},{10,... | collective-permute-start | bytes 3538952 | tf_op jit(solution)/shard_map/ppermute | solution.py:541
  336.6 27.2 %collective-permute-start.48 = (bf16[256,768]{1,0:T(8,128)(2,1)S(1)}, bf16[256,768]{1,0:T(8,128)(2,1)S(1)}, u32[]{:S(2)}, u32[]{:S(2)}) collective-permute-start(bf16[256,768]{1,0:T(8,128)(2,1)S(1)} %convert_element_type.347), channel_id=1, source_target_pairs={{0,2},{1,3},{2,0},{3,1},{4,6},{5,7},{6,4},{7,5},{8,10},{9,11},{10,... | collective-permute-start | bytes 1179656 | tf_op jit(solution)/shard_map/ppermute | solution.py:541
  339.6 30.8 %collective-permute-start.87 = (bf16[384,1536]{0,1:T(8,128)(2,1)S(1)}, bf16[384,1536]{0,1:T(8,128)(2,1)S(1)}, u32[]{:S(2)}, u32[]{:S(2)}) collective-permute-start(bf16[384,1536]{0,1:T(8,128)(2,1)S(1)} %slice.911), channel_id=1, source_target_pairs={{0,4},{4,0},{1,5},{5,1},{2,6},{6,2},{3,7},{7,3},{8,12},{12,8},{9,1... | collective-permute-start | bytes 3538952 | tf_op jit(solution)/shard_map/ppermute | solution.py:541
  363.8 34.8 %collective-permute-start.49 = (bf16[512,768]{1,0:T(8,128)(2,1)S(1)}, bf16[512,768]{1,0:T(8,128)(2,1)S(1)}, u32[]{:S(2)}, u32[]{:S(2)}) collective-permute-start(bf16[512,768]{1,0:T(8,128)(2,1)S(1)} %pad_maximum_fusion.15), channel_id=1, source_target_pairs={{0,1},{1,0},{2,3},{3,2},{4,5},{5,4},{6,7},{7,6},{8,9},{9,8},{10,11... | collective-permute-start | bytes 2359304 | tf_op jit(solution)/shard_map/ppermute | solution.py:541
  366.1 25.2 %collective-permute-start.95 = (bf16[192,768]{0,1:T(8,128)(2,1)S(1)}, bf16[192,768]{0,1:T(8,128)(2,1)S(1)}, u32[]{:S(2)}, u32[]{:S(2)}) collective-permute-start(bf16[192,768]{0,1:T(8,128)(2,1)S(1)} %pad_maximum_fusion.63), channel_id=1, source_target_pairs={{0,16},{8,24},{16,0},{24,8},{1,17},{9,25},{17,1},{25,9},{2,18},{10... | collective-permute-start | bytes 884744 | tf_op jit(solution)/shard_map/ppermute | solution.py:558
  366.3 24.9 %collective-permute-start.96 = (bf16[192,768]{0,1:T(8,128)(2,1)S(1)}, bf16[192,768]{0,1:T(8,128)(2,1)S(1)}, u32[]{:S(2)}, u32[]{:S(2)}) collective-permute-start(bf16[192,768]{0,1:T(8,128)(2,1)S(1)} %pad_maximum_fusion.64), channel_id=1, source_target_pairs={{0,8},{8,16},{16,24},{24,0},{1,9},{9,17},{17,25},{25,1},{2,10},{10... | collective-permute-start | bytes 884744 | tf_op jit(solution)/shard_map/ppermute | solution.py:558
  366.6 29.5 %collective-permute-start.94 = (bf16[192,768]{0,1:T(8,128)(2,1)S(1)}, bf16[192,768]{0,1:T(8,128)(2,1)S(1)}, u32[]{:S(2)}, u32[]{:S(2)}) collective-permute-start(bf16[192,768]{0,1:T(8,128)(2,1)S(1)} %pad_maximum_fusion.62), channel_id=1, source_target_pairs={{0,24},{8,0},{16,8},{24,16},{1,25},{9,1},{17,9},{25,17},{2,26},{10... | collective-permute-start | bytes 884744 | tf_op jit(solution)/shard_map/ppermute | solution.py:558
  371.7 55.2 %collective-permute-start.88 = (bf16[384,768]{0,1:T(8,128)(2,1)}, bf16[384,768]{0,1:T(8,128)(2,1)}, u32[]{:S(2)}, u32[]{:S(2)}) collective-permute-start(bf16[384,768]{0,1:T(8,128)(2,1)} %slice.1153), channel_id=1, source_target_pairs={{0,2},{1,3},{2,0},{3,1},{4,6},{5,7},{6,4},{7,5},{8,10},{9,11},{10,... | collective-permute-start | bytes 1769480 | tf_op jit(solution)/shard_map/ppermute | solution.py:541
  398.1 23.1 %collective-permute-start.97 = (bf16[192,768]{0,1:T(8,128)(2,1)}, bf16[192,768]{0,1:T(8,128)(2,1)}, u32[]{:S(2)}, u32[]{:S(2)}) collective-permute-start(bf16[192,768]{0,1:T(8,128)(2,1)} %pad_maximum_fusion.65), channel_id=1, source_target_pairs={{0,4},{4,0},{1,5},{5,1},{2,6},{6,2},{3,7},{7,3},{8,12},{12,8},{9,1... | collective-permute-start | bytes 884744 | tf_op jit(solution)/shard_map/ppermute | solution.py:541
  418.0 16.3 %collective-permute-start.82 = (bf16[384,768]{0,1:T(8,128)(2,1)}, bf16[384,768]{0,1:T(8,128)(2,1)}, u32[]{:S(2)}, u32[]{:S(2)}) collective-permute-start(bf16[384,768]{0,1:T(8,128)(2,1)} %pad_maximum_fusion.42), channel_id=1, source_target_pairs={{0,4},{4,0},{1,5},{5,1},{2,6},{6,2},{3,7},{7,3},{8,12},{12,8},{9,1... | collective-permute-start | bytes 1769480 | tf_op jit(solution)/shard_map/ppermute | solution.py:541
  421.2 17.6 %collective-permute-start.50 = (bf16[512,768]{1,0:T(8,128)(2,1)}, bf16[512,768]{1,0:T(8,128)(2,1)}, u32[]{:S(2)}, u32[]{:S(2)}) collective-permute-start(bf16[512,768]{1,0:T(8,128)(2,1)} %convolution_convert_fusion.7), channel_id=1, source_target_pairs={{0,1},{1,0},{2,3},{3,2},{4,5},{5,4},{6,7},{7,6},{8,9},{9,8},{10,11... | collective-permute-start | bytes 2359304 | tf_op jit(solution)/shard_map/ppermute | solution.py:541
  429.5 18.5 %collective-permute-start.91 = (bf16[96,768]{0,1:T(8,128)(2,1)S(1)}, bf16[96,768]{0,1:T(8,128)(2,1)S(1)}, u32[]{:S(2)}, u32[]{:S(2)}) collective-permute-start(bf16[96,768]{0,1:T(8,128)(2,1)S(1)} %get-tuple-element.230), channel_id=1, source_target_pairs={{0,8},{8,16},{16,24},{24,0},{1,9},{9,17},{17,25},{25,1},{2,10},{10... | collective-permute-start | bytes 442376 | tf_op jit(solution)/shard_map/ppermute | solution.py:558
  433.0 28.1 %collective-permute-start.90 = (bf16[96,768]{0,1:T(8,128)(2,1)S(1)}, bf16[96,768]{0,1:T(8,128)(2,1)S(1)}, u32[]{:S(2)}, u32[]{:S(2)}) collective-permute-start(bf16[96,768]{0,1:T(8,128)(2,1)S(1)} %get-tuple-element.231), channel_id=1, source_target_pairs={{0,16},{8,24},{16,0},{24,8},{1,17},{9,25},{17,1},{25,9},{2,18},{10... | collective-permute-start | bytes 442376 | tf_op jit(solution)/shard_map/ppermute | solution.py:558
  435.8 26.0 %collective-permute-start.83 = (bf16[96,768]{0,1:T(8,128)(2,1)S(1)}, bf16[96,768]{0,1:T(8,128)(2,1)S(1)}, u32[]{:S(2)}, u32[]{:S(2)}) collective-permute-start(bf16[96,768]{0,1:T(8,128)(2,1)S(1)} %get-tuple-element.232), channel_id=1, source_target_pairs={{0,24},{8,0},{16,8},{24,16},{1,25},{9,1},{17,9},{25,17},{2,26},{10... | collective-permute-start | bytes 442376 | tf_op jit(solution)/shard_map/ppermute | solution.py:558
  438.8 23.0 %collective-permute-start.85 = (bf16[96,768]{0,1:T(8,128)(2,1)S(1)}, bf16[96,768]{0,1:T(8,128)(2,1)S(1)}, u32[]{:S(2)}, u32[]{:S(2)}) collective-permute-start(bf16[96,768]{0,1:T(8,128)(2,1)S(1)} %get-tuple-element.233), channel_id=1, source_target_pairs={{0,8},{8,16},{16,24},{24,0},{1,9},{9,17},{17,25},{25,1},{2,10},{10... | collective-permute-start | bytes 442376 | tf_op jit(solution)/shard_map/ppermute | solution.py:558
  441.1 28.1 %collective-permute-start.84 = (bf16[96,768]{0,1:T(8,128)(2,1)S(1)}, bf16[96,768]{0,1:T(8,128)(2,1)S(1)}, u32[]{:S(2)}, u32[]{:S(2)}) collective-permute-start(bf16[96,768]{0,1:T(8,128)(2,1)S(1)} %get-tuple-element.234), channel_id=1, source_target_pairs={{0,16},{8,24},{16,0},{24,8},{1,17},{9,25},{17,1},{25,9},{2,18},{10... | collective-permute-start | bytes 442376 | tf_op jit(solution)/shard_map/ppermute | solution.py:558
  448.0 21.8 %collective-permute-start.51 = (bf16[256,768]{1,0:T(8,128)(2,1)S(1)}, bf16[256,768]{1,0:T(8,128)(2,1)S(1)}, u32[]{:S(2)}, u32[]{:S(2)}) collective-permute-start(bf16[256,768]{1,0:T(8,128)(2,1)S(1)} %slice.1156), channel_id=1, source_target_pairs={{0,2},{1,3},{2,0},{3,1},{4,6},{5,7},{6,4},{7,5},{8,10},{9,11},{10,... | collective-permute-start | bytes 1179656 | tf_op jit(solution)/shard_map/ppermute | solution.py:541
  486.2 20.3 %collective-permute-start.61 = (f32[2,768]{1,0:T(2,128)S(1)}, f32[2,768]{1,0:T(2,128)S(1)}, u32[]{:S(2)}, u32[]{:S(2)}) collective-permute-start(f32[2,768]{1,0:T(2,128)S(1)} %pad_maximum_fusion.68), channel_id=1, source_target_pairs={{0,2},{1,3},{2,0},{3,1},{4,6},{5,7},{6,4},{7,5},{8,10},{9,11},{10,... | collective-permute-start | bytes 18440 | tf_op jit(solution)/shard_map/ppermute | solution.py:541
  498.3 38.3 %collective-permute-start.77 = (bf16[768,768]{0,1:T(8,128)(2,1)}, bf16[768,768]{0,1:T(8,128)(2,1)}, u32[]{:S(2)}, u32[]{:S(2)}) collective-permute-start(bf16[768,768]{0,1:T(8,128)(2,1)} %slice.882), channel_id=1, source_target_pairs={{0,2},{1,3},{2,0},{3,1},{4,6},{5,7},{6,4},{7,5},{8,10},{9,11},{10,... | collective-permute-start | bytes 3538952 | tf_op jit(solution)/shard_map/ppermute | solution.py:541
  498.9 44.3 %collective-permute-start.71 = (bf16[384,1536]{0,1:T(8,128)(2,1)}, bf16[384,1536]{0,1:T(8,128)(2,1)}, u32[]{:S(2)}, u32[]{:S(2)}) collective-permute-start(bf16[384,1536]{0,1:T(8,128)(2,1)} %slice.873), channel_id=1, source_target_pairs={{0,4},{4,0},{1,5},{5,1},{2,6},{6,2},{3,7},{7,3},{8,12},{12,8},{9,1... | collective-permute-start | bytes 3538952 | tf_op jit(solution)/shard_map/ppermute | solution.py:541
  505.1 30.3 %collective-permute-start.54 = (bf16[256,768]{1,0:T(8,128)(2,1)}, bf16[256,768]{1,0:T(8,128)(2,1)}, u32[]{:S(2)}, u32[]{:S(2)}) collective-permute-start(bf16[256,768]{1,0:T(8,128)(2,1)} %convert_element_type.356), channel_id=1, source_target_pairs={{0,2},{1,3},{2,0},{3,1},{4,6},{5,7},{6,4},{7,5},{8,10},{9,11},{10,... | collective-permute-start | bytes 1179656 | tf_op jit(solution)/shard_map/ppermute | solution.py:541
  536.5 34.9 %collective-permute-start.55 = (bf16[512,768]{1,0:T(8,128)(2,1)S(1)}, bf16[512,768]{1,0:T(8,128)(2,1)S(1)}, u32[]{:S(2)}, u32[]{:S(2)}) collective-permute-start(bf16[512,768]{1,0:T(8,128)(2,1)S(1)} %pad_maximum_fusion.17), channel_id=1, source_target_pairs={{0,1},{1,0},{2,3},{3,2},{4,5},{5,4},{6,7},{7,6},{8,9},{9,8},{10,11... | collective-permute-start | bytes 2359304 | tf_op jit(solution)/shard_map/ppermute | solution.py:541
  538.8 25.2 %collective-permute-start.79 = (bf16[192,768]{0,1:T(8,128)(2,1)S(1)}, bf16[192,768]{0,1:T(8,128)(2,1)S(1)}, u32[]{:S(2)}, u32[]{:S(2)}) collective-permute-start(bf16[192,768]{0,1:T(8,128)(2,1)S(1)} %pad_maximum_fusion.59), channel_id=1, source_target_pairs={{0,16},{8,24},{16,0},{24,8},{1,17},{9,25},{17,1},{25,9},{2,18},{10... | collective-permute-start | bytes 884744 | tf_op jit(solution)/shard_map/ppermute | solution.py:558
  539.1 25.0 %collective-permute-start.80 = (bf16[192,768]{0,1:T(8,128)(2,1)S(1)}, bf16[192,768]{0,1:T(8,128)(2,1)S(1)}, u32[]{:S(2)}, u32[]{:S(2)}) collective-permute-start(bf16[192,768]{0,1:T(8,128)(2,1)S(1)} %pad_maximum_fusion.60), channel_id=1, source_target_pairs={{0,8},{8,16},{16,24},{24,0},{1,9},{9,17},{17,25},{25,1},{2,10},{10... | collective-permute-start | bytes 884744 | tf_op jit(solution)/shard_map/ppermute | solution.py:558
  539.4 29.5 %collective-permute-start.78 = (bf16[192,768]{0,1:T(8,128)(2,1)S(1)}, bf16[192,768]{0,1:T(8,128)(2,1)S(1)}, u32[]{:S(2)}, u32[]{:S(2)}) collective-permute-start(bf16[192,768]{0,1:T(8,128)(2,1)S(1)} %pad_maximum_fusion.58), channel_id=1, source_target_pairs={{0,24},{8,0},{16,8},{24,16},{1,25},{9,1},{17,9},{25,17},{2,26},{10... | collective-permute-start | bytes 884744 | tf_op jit(solution)/shard_map/ppermute | solution.py:558
  545.7 56.5 %collective-permute-start.72 = (bf16[384,768]{0,1:T(8,128)(2,1)}, bf16[384,768]{0,1:T(8,128)(2,1)}, u32[]{:S(2)}, u32[]{:S(2)}) collective-permute-start(bf16[384,768]{0,1:T(8,128)(2,1)} %slice.1154), channel_id=1, source_target_pairs={{0,2},{1,3},{2,0},{3,1},{4,6},{5,7},{6,4},{7,5},{8,10},{9,11},{10,... | collective-permute-start | bytes 1769480 | tf_op jit(solution)/shard_map/ppermute | solution.py:541
  570.9 25.6 %collective-permute-start.81 = (bf16[192,768]{0,1:T(8,128)(2,1)}, bf16[192,768]{0,1:T(8,128)(2,1)}, u32[]{:S(2)}, u32[]{:S(2)}) collective-permute-start(bf16[192,768]{0,1:T(8,128)(2,1)} %pad_maximum_fusion.61), channel_id=1, source_target_pairs={{0,4},{4,0},{1,5},{5,1},{2,6},{6,2},{3,7},{7,3},{8,12},{12,8},{9,1... | collective-permute-start | bytes 884744 | tf_op jit(solution)/shard_map/ppermute | solution.py:541
  593.3 18.0 %collective-permute-start.66 = (bf16[384,768]{0,1:T(8,128)(2,1)}, bf16[384,768]{0,1:T(8,128)(2,1)}, u32[]{:S(2)}, u32[]{:S(2)}) collective-permute-start(bf16[384,768]{0,1:T(8,128)(2,1)} %pad_maximum_fusion.43), channel_id=1, source_target_pairs={{0,4},{4,0},{1,5},{5,1},{2,6},{6,2},{3,7},{7,3},{8,12},{12,8},{9,1... | collective-permute-start | bytes 1769480 | tf_op jit(solution)/shard_map/ppermute | solution.py:541
  596.5 48.7 %collective-permute-start.56 = (bf16[512,768]{1,0:T(8,128)(2,1)}, bf16[512,768]{1,0:T(8,128)(2,1)}, u32[]{:S(2)}, u32[]{:S(2)}) collective-permute-start(bf16[512,768]{1,0:T(8,128)(2,1)} %convolution_convert_fusion.6), channel_id=1, source_target_pairs={{0,1},{1,0},{2,3},{3,2},{4,5},{5,4},{6,7},{7,6},{8,9},{9,8},{10,11... | collective-permute-start | bytes 2359304 | tf_op jit(solution)/shard_map/ppermute | solution.py:541
  608.3 19.7 %collective-permute-start.74 = (bf16[96,768]{0,1:T(8,128)(2,1)S(1)}, bf16[96,768]{0,1:T(8,128)(2,1)S(1)}, u32[]{:S(2)}, u32[]{:S(2)}) collective-permute-start(bf16[96,768]{0,1:T(8,128)(2,1)S(1)} %get-tuple-element.237), channel_id=1, source_target_pairs={{0,16},{8,24},{16,0},{24,8},{1,17},{9,25},{17,1},{25,9},{2,18},{10... | collective-permute-start | bytes 442376 | tf_op jit(solution)/shard_map/ppermute | solution.py:558
  614.2 19.2 %collective-permute-start.69 = (bf16[96,768]{0,1:T(8,128)(2,1)S(1)}, bf16[96,768]{0,1:T(8,128)(2,1)S(1)}, u32[]{:S(2)}, u32[]{:S(2)}) collective-permute-start(bf16[96,768]{0,1:T(8,128)(2,1)S(1)} %get-tuple-element.239), channel_id=1, source_target_pairs={{0,8},{8,16},{16,24},{24,0},{1,9},{9,17},{17,25},{25,1},{2,10},{10... | collective-permute-start | bytes 442376 | tf_op jit(solution)/shard_map/ppermute | solution.py:558
  620.7 23.9 %collective-permute-start.68 = (bf16[96,768]{0,1:T(8,128)(2,1)S(1)}, bf16[96,768]{0,1:T(8,128)(2,1)S(1)}, u32[]{:S(2)}, u32[]{:S(2)}) collective-permute-start(bf16[96,768]{0,1:T(8,128)(2,1)S(1)} %get-tuple-element.240), channel_id=1, source_target_pairs={{0,16},{8,24},{16,0},{24,8},{1,17},{9,25},{17,1},{25,9},{2,18},{10... | collective-permute-start | bytes 442376 | tf_op jit(solution)/shard_map/ppermute | solution.py:558
  628.2 21.1 %collective-permute-start.76 = (bf16[96,768]{0,1:T(8,128)(2,1)S(1)}, bf16[96,768]{0,1:T(8,128)(2,1)S(1)}, u32[]{:S(2)}, u32[]{:S(2)}) collective-permute-start(bf16[96,768]{0,1:T(8,128)(2,1)S(1)} %fusion.78), channel_id=1, source_target_pairs={{0,4},{4,0},{1,5},{5,1},{2,6},{6,2},{3,7},{7,3},{8,12},{12,8},{9,1... | collective-permute-start | bytes 442376 | tf_op jit(solution)/shard_map/ppermute | solution.py:541
  (195 other events, 2285.9 us)
